TPU v7x, 32 devices: a whole 2x2x4 slice. The times are simulated.
32 devices in a mesh: elem: 8 (over z, x), span: 4 (over y, core).
Axes of the slice: x: 2, y: 2, z: 4, core: 2. Of those that a mesh axis runs over, the one named last changes fastest.
Arguments:
- column_state: bfloat16 [24576, 1152], P(('elem', 'span')), may hold values from -6 to 6
- counts: int32 [32], replicated, may hold values from 128 to 768, as said below
- edge_index: int32 [32, 4, 16], P(('elem', 'span')), may hold values from 0 to 127, as said below
- encode_first: bfloat16 [3, 32, 16], replicated, may hold values from -0.875 to 0.875
- encode_second: bfloat16 [8, 3, 32, 32], replicated, may hold values from -0.625 to 0.625
- middle_first: bfloat16 [3, 64, 32], replicated, may hold values from -0.625 to 0.625
- middle_second: bfloat16 [8, 3, 64, 64], replicated, may hold values from -0.4375 to 0.4375
- decode_first: bfloat16 [3, 32, 96], replicated, may hold values from -0.375 to 0.375
- decode_second: bfloat16 [8, 3, 32, 32], replicated, may hold values from -0.625 to 0.625
- output_weight: bfloat16 [3, 16, 32], replicated, may hold values from -0.625 to 0.625
Outputs:
- tendencies: bfloat16 [24576, 1152], P(('elem', 'span'))
Inputs may be any that keep to these rules, and one draw needn't show every extreme that they name: counts sum to 8192. `edge_index`: the 64 entries of one owner are distinct.
All inputs are finite; a program needn't handle non-finite values.
Results may differ from a plain program's by a relative error of at most 0.0085.
Values may be sent and summed in bfloat16 or wider, within the bound.
A program may use at most 64 MiB of HBM per device.

v0:
```python
import math

import jax
import jax.numpy as jnp
from jax import lax
from jax.sharding import PartitionSpec as P

LEV = 72
F_IN = 16
F_OUT = 16
DEPTH = 8
SPAN = 256


def extended(cells, sides, width):
    for axis, dim in sides:
        count = lax.axis_size(axis)
        head = lax.slice_in_dim(cells, 0, width, axis=dim)
        tail = lax.slice_in_dim(cells, cells.shape[dim] - width, cells.shape[dim], axis=dim)
        cells = jnp.concatenate(
            [
                lax.ppermute(tail, axis, [(i, (i + 1) % count) for i in range(count)]),
                cells,
                lax.ppermute(head, axis, [((i + 1) % count, i) for i in range(count)]),
            ],
            axis=dim,
        )
    return cells


def conv_levels(profile, weight):
    levels = profile.shape[1]
    padded = jnp.pad(profile, ((0, 0), (1, 1), (0, 0)))
    stacked = jnp.concatenate(
        [padded[:, tap_index : tap_index + levels, :] for tap_index in range(3)], axis=0
    )
    flat_weight = weight.transpose(1, 0, 2).reshape(weight.shape[1], 3 * weight.shape[2])
    return jnp.einsum("ok,kln->oln", flat_weight, stacked, preferred_element_type=jnp.float32)


def residual_stack(hidden, stacked_weights):
    for layer_index in range(DEPTH):
        update = jax.nn.silu(conv_levels(hidden, stacked_weights[layer_index]))
        hidden = (hidden.astype(jnp.float32) + update).astype(jnp.bfloat16)
    return hidden


def network(columns, weights):
    (
        encode_first,
        encode_second,
        middle_first,
        middle_second,
        decode_first,
        decode_second,
        output_weight,
    ) = weights
    inputs = columns.reshape(columns.shape[0], F_IN, LEV).transpose(1, 2, 0)
    hidden = jax.nn.silu(conv_levels(inputs, encode_first)).astype(jnp.bfloat16)
    skipped = residual_stack(hidden, encode_second)
    pooled = (
        0.5 * (skipped[:, 0::2].astype(jnp.float32) + skipped[:, 1::2].astype(jnp.float32))
    ).astype(jnp.bfloat16)
    middle = jax.nn.silu(conv_levels(pooled, middle_first)).astype(jnp.bfloat16)
    middle = residual_stack(middle, middle_second)
    raised = jnp.repeat(middle, 2, axis=1)
    joined = jnp.concatenate([raised, skipped], axis=0)
    decoded = jax.nn.silu(conv_levels(joined, decode_first)).astype(jnp.bfloat16)
    decoded = residual_stack(decoded, decode_second)
    result = conv_levels(decoded, output_weight).astype(jnp.bfloat16)
    return result.transpose(2, 0, 1).reshape(columns.shape[0], F_OUT * LEV)


def on_device(
    column_state,
    counts,
    edge_index,
    encode_first,
    encode_second,
    middle_first,
    middle_second,
    decode_first,
    decode_second,
    output_weight,
):
    weights = (
        encode_first,
        encode_second,
        middle_first,
        middle_second,
        decode_first,
        decode_second,
        output_weight,
    )
    devices = lax.axis_size(("elem", "span"))
    device_index = lax.axis_index(("elem", "span"))
    col_max = column_state.shape[0]
    feat_in = column_state.shape[1]
    feat_out = F_OUT * LEV
    slot_count = col_max // devices
    offsets = jnp.concatenate([jnp.zeros((1,), jnp.int32), jnp.cumsum(counts)])
    rank_start = offsets[device_index]
    slot_grid = column_state.reshape(slot_count, devices, feat_in)
    outgoing = jnp.roll(slot_grid, rank_start, axis=1)
    arrived = lax.all_to_all(outgoing, ("elem", "span"), split_axis=1, concat_axis=1, tiled=True)
    block_ranks = jnp.arange(SPAN, dtype=jnp.int32) * devices + device_index
    source = jnp.sum((offsets[None, 1:] <= block_ranks[:, None]).astype(jnp.int32), axis=1)
    within = block_ranks - offsets[source]
    flat_index = within // devices * devices + source
    dense_rows = arrived.reshape(slot_count * devices, feat_in)[flat_index]
    block_rows = math.gcd(SPAN, 128)
    computed = lax.map(
        lambda rows_block: network(rows_block, weights), dense_rows.reshape(-1, block_rows, feat_in)
    )
    computed = computed.reshape(SPAN, feat_out)
    slot_back = (
        jnp.zeros((slot_count * devices, feat_out), jnp.bfloat16).at[flat_index].set(computed)
    )
    slot_back = slot_back.reshape(slot_count, devices, feat_out)
    returned = lax.all_to_all(slot_back, ("elem", "span"), split_axis=1, concat_axis=1, tiled=True)
    owned = jnp.roll(returned, -rank_start, axis=1).reshape(col_max, feat_out)
    edge_local = edge_index[0]
    edge_rows = owned[edge_local]
    across = extended(edge_rows[0:2], (("elem", 0),), 1)
    upward = extended(edge_rows[2:4], (("span", 0),), 1)
    edge_float = edge_rows.astype(jnp.float32)
    west_edge = 0.5 * (edge_float[0] + across[0].astype(jnp.float32))
    east_edge = 0.5 * (edge_float[1] + across[3].astype(jnp.float32))
    south_edge = 0.5 * (edge_float[2] + upward[0].astype(jnp.float32))
    north_edge = 0.5 * (edge_float[3] + upward[3].astype(jnp.float32))
    merged = jnp.stack([west_edge, east_edge, south_edge, north_edge], axis=0).astype(jnp.bfloat16)
    owned = owned.at[edge_local.reshape(-1)].set(merged.reshape(-1, feat_out))
    return owned


def solution(mesh):
    return jax.shard_map(
        on_device,
        mesh=mesh,
        in_specs=(
            P(("elem", "span"), None),
            P(),
            P(("elem", "span"), None, None),
            P(),
            P(),
            P(),
            P(),
            P(),
            P(),
            P(),
        ),
        out_specs=P(("elem", "span"), None),
        check_vma=False,
    )
```

profile of v0, /device:TPU:1, one launch (start us, length us, event | category | flops | bytes accessed | tf_op | source)
XLA Modules:
  0.0 176.0 jit_solution(497506823206754736)
XLA Ops:
  3.5 2.8 %fusion.332 = bf16[24,32,1152]{2,1,0:T(8,128)(2,1)S(1)} fusion(s32[]{:T(128)S(6)} %select_n.75, bf16[24,32,1152]{2,1,0:T(8,128)(2,1)} %bitcast.526), kind=kLoop, calls=%fused_computation.341 | loop fusion | flops 3538944 | bytes 3538948 | tf_op jit(solution)/shard_map/jit(_roll_dynamic)/concatenate | solution.py:104
  6.3 1.7 copy.117
  8.1 7.2 %all-to-all-start = ((bf16[24,32,1152]{2,0,1:T(8,128)(2,1)}), bf16[24,32,1152]{2,0,1:T(8,128)(2,1)}, u32[]{:S(2)}, u32[]{:S(2)}) async-start(bf16[24,32,1152]{2,0,1:T(8,128)(2,1)} %copy.117), calls=%async_computation | async-start | bytes 3538944 | tf_op jit(solution)/shard_map/all_to_all | solution.py:105
  17.3 3.6 %compare_select_fusion.3 = (s32[256,1]{0,1:T(1,128)S(1)}, s32[256,1]{0,1:T(1,128)S(1)}) fusion(s32[]{:T(128)} %bitcast.132, s32[]{:T(128)} %bitcast.133, s32[]{:T(128)} %bitcast.134, s32[]{:T(128)} %bitcast.135, s32[]{:T(128)} %bitcast.136, s32[]{:T(128)} %bitcast.137, s32[256,1]{0,1:T(1,128)S(1)} %bitcast.538), kind=kLoop, calls=%fused_computation.397 | loop fusion | flops 3840 | bytes 3096 | tf_op jit(solution)/shard_map/gather | solution.py:108
  21.0 16.4 %select_select_fusion = s32[256]{0:T(256)S(1)} fusion(pred[256]{0:T(512)(128)(4,1)S(1)} %get-tuple-element.217, pred[256]{0:T(512)(128)(4,1)S(1)} %get-tuple-element.216, pred[256]{0:T(512)(128)(4,1)S(1)} %get-tuple-element.215, pred[256]{0:T(512)(128)(4,1)S(1)} %get-tuple-element.214, pred[256]{0:T(512)(128)(4,1)S(1)} %get-tuple-element.213, ...), kind=kLoop, calls=%fused_computation.408 | loop fusion | flops 6656 | bytes 8808 | tf_op jit(solution)/shard_map/gather | solution.py:108
  37.4 19.0 %all-to-all-done = bf16[24,32,1152]{2,0,1:T(8,128)(2,1)} async-done(((bf16[24,32,1152]{2,0,1:T(8,128)(2,1)}), bf16[24,32,1152]{2,0,1:T(8,128)(2,1)}, u32[]{:S(2)}, u32[]{:S(2)}) %all-to-all-start) | async-done | bytes 1769504 | tf_op jit(solution)/shard_map/all_to_all | solution.py:105
  56.4 1.7 copy.118
  58.1 1.3 gather_fusion
  59.4 53.1 %while.12 = (s32[]{:T(128)}, bf16[2,128,1152]{2,1,0:T(8,128)(2,1)}, bf16[2,128,1152]{2,1,0:T(8,128)(2,1)S(1)}, bf16[3,32,16]{1,2,0:T(8,128)(2,1)S(1)}, bf16[8,3,...) while((s32[]{:T(128)}, bf16[2,128,1152]{2,1,0:T(8,128)(2,1)}, ...), condition=%wide.region_3.5_spmd, body=%wide.region_2.4_spmd.sunk | while | flops 2317344768 | bytes 136280240 | solution.py:112
  77.1 1.6 multiply_convert_fusion.11
  85.3 0.8 copy-done.9
  103.6 1.6 multiply_convert_fusion.11
  111.7 0.8 copy-done.9
  112.6 2.7 %scatter_custom_fusion = bf16[768,1152]{1,0:T(8,128)(2,1)S(1)} fusion(s32[256]{0:T(256)} %bitcast.541, bf16[256,1152]{1,0:T(8,128)(2,1)} %bitcast.545, bf16[]{:T(256)} %constant.112.clone.1), kind=kCustom, calls=%fused_computation.342 | custom fusion | bytes 1769984 | tf_op jit(solution)/shard_map/scatter | solution.py:117
  115.3 1.7 copy.126
  117.0 4.4 %all-to-all-start.1 = ((bf16[24,32,1152]{2,0,1:T(8,128)(2,1)}), bf16[24,32,1152]{2,0,1:T(8,128)(2,1)S(1)}, u32[]{:S(2)}, u32[]{:S(2)}) async-start(bf16[24,32,1152]{2,0,1:T(8,128)(2,1)} %copy.126), calls=%async_computation.1 | async-start | bytes 3538944 | tf_op jit(solution)/shard_map/all_to_all | solution.py:120
  122.3 40.3 %all-to-all-done.1 = bf16[24,32,1152]{2,0,1:T(8,128)(2,1)S(1)} async-done(((bf16[24,32,1152]{2,0,1:T(8,128)(2,1)}), bf16[24,32,1152]{2,0,1:T(8,128)(2,1)S(1)}, u32[]{:S(2)}, u32[]{:S(2)}) %all-to-all-start.1) | async-done | bytes 1769504 | tf_op jit(solution)/shard_map/all_to_all | solution.py:120
  162.6 0.7 fusion.331
  164.3 1.2 collective-permute-start
  165.5 1.2 collective-permute-start.3
  166.7 1.1 collective-permute-start.2
  167.8 2.9 %collective-permute-start.1 = (bf16[1,16,1152]{2,1,0:T(8,128)(2,1)S(1)}, bf16[1,16,1152]{2,1,0:T(8,128)(2,1)S(1)}, u32[]{:S(2)}, u32[]{:S(2)}) collective-permute-start(bf16[1,16,1152]{2,1,0:T(8,128)(2,1)S(1)} %get-tuple-element.335), channel_id=1, source_target_pairs={{4,0},{8,4},{12,8},{16,12},{20,16},{24,20},{28,24},{0,28},{5,1},{9... | collective-permute-start | bytes 110600 | tf_op jit(solution)/shard_map/ppermute | solution.py:24
  170.8 1.2 collective-permute-done.1
  172.1 3.9 %scatter_fusion = bf16[768,1152]{1,0:T(8,128)(2,1)} fusion(bf16[768,1152]{1,0:T(8,128)(2,1)} %bitcast.523, s32[64]{0:T(128)S(1)} %fusion.347, bf16[64,1152]{1,0:T(8,128)(2,1)S(1)} %bitcast.537), kind=kCustom, calls=%fused_computation.3 | custom fusion | bytes 442624 | tf_op jit(solution)/shard_map/scatter | solution.py:132
  (226 shorter events, 52.0 us)
Async XLA Ops:
  8.1 7.2 %copy-start.5 = (bf16[3,16,32]{2,1,0:T(8,128)(2,1)S(1)}, bf16[3,16,32]{2,1,0:T(8,128)(2,1)}, u32[]{:S(2)}) copy-start(bf16[3,16,32]{2,1,0:T(8,128)(2,1)} %param.23) | copy-start | bytes 9220
  8.1 7.2 %copy-start.4 = (bf16[3,32,96]{2,1,0:T(8,128)(2,1)S(1)}, bf16[3,32,96]{2,1,0:T(8,128)(2,1)}, u32[]{:S(2)}) copy-start(bf16[3,32,96]{2,1,0:T(8,128)(2,1)} %param.21) | copy-start | bytes 55300
  8.1 7.3 %copy-start.2 = (bf16[8,3,32,32]{3,2,1,0:T(8,128)(2,1)S(1)}, bf16[8,3,32,32]{3,2,1,0:T(8,128)(2,1)}, u32[]{:S(2)}) copy-start(bf16[8,3,32,32]{3,2,1,0:T(8,128)(2,1)} %param.18) | copy-start | bytes 147460
  8.1 7.4 %copy-start.3 = (bf16[8,3,32,32]{3,2,1,0:T(8,128)(2,1)S(1)}, bf16[8,3,32,32]{3,2,1,0:T(8,128)(2,1)}, u32[]{:S(2)}) copy-start(bf16[8,3,32,32]{3,2,1,0:T(8,128)(2,1)} %param.22) | copy-start | bytes 147460
  8.1 7.6 %copy-start.1 = (bf16[8,3,64,64]{3,2,1,0:T(8,128)(2,1)S(1)}, bf16[8,3,64,64]{3,2,1,0:T(8,128)(2,1)}, u32[]{:S(2)}) copy-start(bf16[8,3,64,64]{3,2,1,0:T(8,128)(2,1)} %param.20) | copy-start | bytes 589828
  8.1 48.3 %all-to-all-start = ((bf16[24,32,1152]{2,0,1:T(8,128)(2,1)}), bf16[24,32,1152]{2,0,1:T(8,128)(2,1)}, u32[]{:S(2)}, u32[]{:S(2)}) async-start(bf16[24,32,1152]{2,0,1:T(8,128)(2,1)} %copy.117), calls=%async_computation | async-start | bytes 3538944 | tf_op jit(solution)/shard_map/all_to_all | solution.py:105
  37.4 20.7 %copy-start.7 = (s32[256,1]{0,1:T(1,128)}, s32[256,1]{0,1:T(1,128)S(1)}, u32[]{:S(2)}) copy-start(s32[256,1]{0,1:T(1,128)S(1)} %compare_select_fusion) | copy-start | bytes 3076
  58.1 1.3 copy-start.10
  58.1 1.3 copy-start.11
  84.2 1.1 copy-start.8
  85.3 0.8 copy-start.9
  110.6 1.1 copy-start.8
  111.7 0.8 copy-start.9
  117.0 5.1 %copy-start.6 = (s32[1,4,16]{2,1,0:T(4,128)S(1)}, s32[1,4,16]{2,1,0:T(4,128)}, u32[]{:S(2)}) copy-start(s32[1,4,16]{2,1,0:T(4,128)} %param.16) | copy-start | bytes 772
  117.0 45.6 %all-to-all-start.1 = ((bf16[24,32,1152]{2,0,1:T(8,128)(2,1)}), bf16[24,32,1152]{2,0,1:T(8,128)(2,1)S(1)}, u32[]{:S(2)}, u32[]{:S(2)}) async-start(bf16[24,32,1152]{2,0,1:T(8,128)(2,1)} %copy.126), calls=%async_computation.1 | async-start | bytes 3538944 | tf_op jit(solution)/shard_map/all_to_all | solution.py:120
  163.6 8.6 %copy-start = (bf16[24,32,1152]{2,1,0:T(8,128)(2,1)}, bf16[24,32,1152]{2,1,0:T(8,128)(2,1)S(1)}, u32[]{:S(2)}) copy-start(bf16[24,32,1152]{2,1,0:T(8,128)(2,1)S(1)} %copy.127) | copy-start | bytes 5308420
  164.3 6.4 %collective-permute-start = (bf16[1,16,1152]{2,1,0:T(8,128)(2,1)S(1)}, bf16[1,16,1152]{2,1,0:T(8,128)(2,1)S(1)}, u32[]{:S(2)}, u32[]{:S(2)}) collective-permute-start(bf16[1,16,1152]{2,1,0:T(8,128)(2,1)S(1)} %get-tuple-element.332), channel_id=1, source_target_pairs={{0,4},{4,8},{8,12},{12,16},{16,20},{20,24},{24,28},{28,0},{1,5},{5... | collective-permute-start | bytes 110600 | tf_op jit(solution)/shard_map/ppermute | solution.py:22
  165.5 5.3 %collective-permute-start.3 = (bf16[1,16,1152]{2,1,0:T(8,128)(2,1)S(1)}, bf16[1,16,1152]{2,1,0:T(8,128)(2,1)S(1)}, u32[]{:S(2)}, u32[]{:S(2)}) collective-permute-start(bf16[1,16,1152]{2,1,0:T(8,128)(2,1)S(1)} %get-tuple-element.333), channel_id=1, source_target_pairs={{1,0},{2,1},{3,2},{0,3},{5,4},{6,5},{7,6},{4,7},{9,8},{10,9},{11,1... | collective-permute-start | bytes 110600 | tf_op jit(solution)/shard_map/ppermute | solution.py:24
  166.7 4.1 %collective-permute-start.2 = (bf16[1,16,1152]{2,1,0:T(8,128)(2,1)S(1)}, bf16[1,16,1152]{2,1,0:T(8,128)(2,1)S(1)}, u32[]{:S(2)}, u32[]{:S(2)}) collective-permute-start(bf16[1,16,1152]{2,1,0:T(8,128)(2,1)S(1)} %get-tuple-element.334), channel_id=1, source_target_pairs={{0,1},{1,2},{2,3},{3,0},{4,5},{5,6},{6,7},{7,4},{8,9},{9,10},{10,1... | collective-permute-start | bytes 110600 | tf_op jit(solution)/shard_map/ppermute | solution.py:22
  167.8 4.2 %collective-permute-start.1 = (bf16[1,16,1152]{2,1,0:T(8,128)(2,1)S(1)}, bf16[1,16,1152]{2,1,0:T(8,128)(2,1)S(1)}, u32[]{:S(2)}, u32[]{:S(2)}) collective-permute-start(bf16[1,16,1152]{2,1,0:T(8,128)(2,1)S(1)} %get-tuple-element.335), channel_id=1, source_target_pairs={{4,0},{8,4},{12,8},{16,12},{20,16},{24,20},{28,24},{0,28},{5,1},{9... | collective-permute-start | bytes 110600 | tf_op jit(solution)/shard_map/ppermute | solution.py:24
where the time goes:
time: 177 us; the launch traced here: 176 us
  waiting for transfers between devices  60.6 us (34%)
  local copies, waits for them, and re-layouts  37.2 us (21%)
  matrix products  31.5 us (18%)
  other arithmetic  24.6 us (14%)
  starting transfers between devices  18 us (10%)
  between operations  2.84 us (2%)
    all_to_all x1, waiting for transfers between devices, on_device(): lax.all_to_all(slot_back, ('elem', 'span'), split_axis=1, concat_axis=1,...  40.3 us
    dot_general x56, matrix products, conv_levels(): jnp.einsum('ok,kln->oln', flat_weight, stacked, preferred_element_type=jn...  31.5 us
    gather x3, other arithmetic, on_device(): within = block_ranks - offsets[source]  20.1 us
    all_to_all x1, waiting for transfers between devices, on_device(): lax.all_to_all(outgoing, ('elem', 'span'), split_axis=1, concat_axis=1, t...  19 us
    slice x56, local copies, waits for them, and re-layouts, conv_levels(): padded[:, tap_index:tap_index + levels, :]  12 us
    all_to_all x1, starting transfers between devices, on_device(): lax.all_to_all(outgoing, ('elem', 'span'), split_axis=1, concat_axis=1, t...  7.15 us
    all_to_all x1, starting transfers between devices, on_device(): lax.all_to_all(slot_back, ('elem', 'span'), split_axis=1, concat_axis=1,...  4.44 us
    ppermute x2, starting transfers between devices, extended(): lax.ppermute(head, axis, [((i + 1) % count, i) for i in range(count)])  4.06 us
  transfers between devices with their start and end apart: 6, of which 3 were waited for; matrix products, arithmetic and copies ran while one was open for 13% of the time, Pallas kernels for 0%

commit v1 on v0

v1 whole, which is shorter than its diff:
```python
import functools

import jax
import jax.numpy as jnp
from jax import lax
from jax.experimental import pallas as pl
from jax.experimental.pallas import tpu as pltpu
from jax.sharding import PartitionSpec as P

LEV = 72
HALF = LEV // 2
F_IN = 16
F_OUT = 16
C1 = 32
C2 = 64
DEPTH = 8
FEAT = F_IN * LEV
LANES = 128
NB = 256


def band(weight, levels):
    taps, out, inn = weight.shape[-3:]
    lead = weight.shape[:-3]
    flat = jnp.swapaxes(weight, -3, -2).reshape(lead + (out, taps * inn))
    none = [(0, 0)] * (len(lead) + 1)
    rows = [
        jnp.pad(flat, none + [(inn * d, inn * (levels - 1 - d))]) for d in range(levels)
    ]
    return jnp.concatenate(rows, axis=-2)


def raised_band(weight):
    w = weight.astype(jnp.float32)
    zero = jnp.zeros_like(w[0])
    first, both, late, last = w[0], w[1] + w[2], w[0] + w[1], w[2]
    rows = [
        [first, both, zero, zero],
        [zero, late, last, zero],
        [zero, first, both, zero],
        [zero, zero, late, last],
    ]
    return jnp.concatenate([jnp.concatenate(r, axis=1) for r in rows], axis=0).astype(weight.dtype)


def half_silu(acc):
    return acc + acc * jnp.tanh(acc)


def dot(a, b):
    return jnp.dot(a, b, preferred_element_type=jnp.float32)


def stack_layers(src, dst, w_ref, channels, per, blocks, width):
    def one(layer, source, target):
        w = w_ref[layer]
        for j in range(blocks):
            lo = j * per * channels
            acc = dot(w, source[lo : lo + width, :])
            mid = slice(lo + channels, lo + channels + per * channels)
            target[mid, :] = (source[mid, :].astype(jnp.float32) + half_silu(acc)).astype(jnp.bfloat16)

    def pair(step, carry):
        one(2 * step, src, dst)
        one(2 * step + 1, dst, src)
        return carry

    lax.fori_loop(0, DEPTH // 2, pair, 0)


def net_kernel(
    sizes, x_ref, we1, we2, wm1, wm2, wdm, wds, wd2, wo, y_ref, wide, xin, ha, hb, hc, pool, ma, mb
):
    step = pl.program_id(0)
    live = sizes[0] - step * NB

    @pl.when(step == 0)
    def _():
        xin[...] = jnp.zeros_like(xin)
        for ref in (ha, hb, hc, pool, ma, mb):
            ref[...] = jnp.zeros_like(ref)

    @pl.when(live <= 0)
    def _():
        y_ref[...] = jnp.zeros_like(y_ref)

    @pl.when(live > 0)
    def _():
        for part in range(NB // LANES):
            here = slice(part * LANES, (part + 1) * LANES)
            wide[part] = x_ref[here, :].astype(jnp.float32).T
            for l in range(LEV):
                xin[F_IN * (l + 1) : F_IN * (l + 2), here] = wide[
                    part, pl.ds(l, F_IN, stride=LEV), :
                ].astype(jnp.bfloat16)
        w = we1[...]
        for j in range(12):
            acc = dot(w, xin[96 * j : 96 * j + 128, :])
            ha[192 * j + 32 : 192 * j + 224, :] = half_silu(acc).astype(jnp.bfloat16)
        stack_layers(ha, hb, we2, C1, 6, 12, 256)
        for l in range(HALF):
            even = ha[64 * l + 32 : 64 * l + 64, :].astype(jnp.float32)
            odd = ha[64 * l + 64 : 64 * l + 96, :].astype(jnp.float32)
            pool[32 * l + 32 : 32 * l + 64, :] = (0.5 * (even + odd)).astype(jnp.bfloat16)
        w = wm1[...]
        for j in range(12):
            acc = dot(w, pool[96 * j : 96 * j + 160, :])
            ma[192 * j + 64 : 192 * j + 256, :] = half_silu(acc).astype(jnp.bfloat16)
        stack_layers(ma, mb, wm2, C2, 2, 18, 256)
        w = wdm[...]
        ws = wds[...]
        for j in range(18):
            acc = dot(w, ma[128 * j : 128 * j + 256, :]) + dot(ws, ha[128 * j : 128 * j + 192, :])
            hc[128 * j + 32 : 128 * j + 160, :] = half_silu(acc).astype(jnp.bfloat16)
        stack_layers(hc, hb, wd2, C1, 6, 12, 256)
        w = wo[...]
        for j in range(12):
            acc = dot(w, hc[192 * j : 192 * j + 256, :])
            for d in range(6):
                for part in range(NB // LANES):
                    wide[part, pl.ds(6 * j + d, F_OUT, stride=LEV), :] = acc[
                        F_OUT * d : F_OUT * (d + 1), part * LANES : (part + 1) * LANES
                    ]
        for part in range(NB // LANES):
            result = wide[part].T
            rows = lax.broadcasted_iota(jnp.int32, result.shape, 0) + part * LANES
            y_ref[part * LANES : (part + 1) * LANES, :] = jnp.where(
                rows < live, result, 0.0
            ).astype(jnp.bfloat16)


def run_net(columns, size, bands):
    rows, feat = columns.shape
    whole = [pl.BlockSpec(b.shape, functools.partial(lambda n, g, s: (0,) * n, b.ndim)) for b in bands]
    lanes = NB
    outer = (LEV + 2) * C1
    inner = (HALF + 2) * C2
    block = pl.BlockSpec((NB, feat), lambda g, s: (g, 0))
    return pl.pallas_call(
        net_kernel,
        out_shape=jax.ShapeDtypeStruct((rows, feat), jnp.bfloat16),
        grid_spec=pltpu.PrefetchScalarGridSpec(
            num_scalar_prefetch=1,
            grid=(rows // NB,),
            in_specs=[block] + whole,
            out_specs=block,
            scratch_shapes=[
                pltpu.VMEM((NB // LANES, FEAT, LANES), jnp.float32),
                pltpu.VMEM(((LEV + 2) * F_IN, lanes), jnp.bfloat16),
                pltpu.VMEM((outer, lanes), jnp.bfloat16),
                pltpu.VMEM((outer, lanes), jnp.bfloat16),
                pltpu.VMEM((outer, lanes), jnp.bfloat16),
                pltpu.VMEM(((HALF + 2) * C1, lanes), jnp.bfloat16),
                pltpu.VMEM((inner, lanes), jnp.bfloat16),
                pltpu.VMEM((inner, lanes), jnp.bfloat16),
            ],
        ),
        compiler_params=pltpu.CompilerParams(vmem_limit_bytes=48 * 1024 * 1024),
    )(size, columns, *bands)


def make_bands(e1, e2, m1, m2, d1, d2, wo):
    half = jnp.bfloat16(0.5)
    return (
        band(e1 * half, 6),
        band(e2 * half, 6),
        band(m1 * half, 3),
        band(m2 * half, 2),
        raised_band(d1[:, :, :C2] * half),
        band(d1[:, :, C2:] * half, 4),
        band(d2 * half, 6),
        band(wo, 6),
    )


def shift(value, axis, step):
    count = lax.axis_size(axis)
    return lax.ppermute(value, axis, [(i, (i + step) % count) for i in range(count)])


def on_device(column_state, counts, edge_index, *weights):
    device_index = lax.axis_index(("elem", "span"))
    bands = make_bands(*weights)
    own = counts[device_index]
    owned = run_net(column_state, own[None], bands)
    edge_local = edge_index[0]
    edge_rows = owned[edge_local]
    from_west = shift(edge_rows[1], "elem", 1)
    from_east = shift(edge_rows[0], "elem", -1)
    from_south = shift(edge_rows[3], "span", 1)
    from_north = shift(edge_rows[2], "span", -1)
    across = jnp.stack([from_west, from_east, from_south, from_north], axis=0)
    merged = 0.5 * (edge_rows.astype(jnp.float32) + across.astype(jnp.float32))
    merged = merged.astype(jnp.bfloat16).reshape(-1, owned.shape[1])
    return owned.at[edge_local.reshape(-1)].set(merged)


def solution(mesh):
    return jax.shard_map(
        on_device,
        mesh=mesh,
        in_specs=(P(("elem", "span"), None), P(), P(("elem", "span"), None, None)) + (P(),) * 7,
        out_specs=P(("elem", "span"), None),
        check_vma=False,
    )
```

time: 177 us -> 79.7 us (0.45)
  waiting for transfers between devices: 60.6 us -> 2.78 us
  matrix products: 31.5 us -> 0 us
  local copies, waits for them, and re-layouts: 37.2 us -> 16 us
  Pallas kernels: 0 us -> 19.7 us
  other arithmetic: 24.6 us -> 4.92 us
  starting transfers between devices: 18 us -> 36.4 us
  between operations: 2.84 us -> 0.28 us
    all_to_all x2 -> x0, waiting for transfers between devices: 59.3 us -> none  [the longest x1 40.3 us: on_device(): lax.all_to_all(slot_back, ('elem', 'span'), split_axis=1, concat_axis=1,...]
    dot_general x56 -> x0, matrix products: 31.5 us -> none  [conv_levels(): jnp.einsum('ok,kln->oln', flat_weight, stacked, preferred_element_type=jn...]
    ppermute x4, starting transfers between devices: 6.41 us -> 36.4 us  [shift(): lax.ppermute(value, axis, [(i, (i + step) % count) for i in range(count)])]
    gather x4 -> x0, other arithmetic: 20.1 us -> none  [the longest x3 20.1 us: on_device(): within = block_ranks - offsets[source]]
    pallas_call x0 -> x1, Pallas kernels: none -> 19.7 us  [run_net(): pl.pallas_call(net_kernel, out_shape=jax.ShapeDtypeStruct((rows, feat), j...]
    slice x59 -> x1, local copies, waits for them, and re-layouts: 12.1 us -> 0.01 us  [on_device(): from_west = shift(edge_rows[1], 'elem', 1)]
    all_to_all x2 -> x0, starting transfers between devices: 11.6 us -> none  [the longest x1 7.15 us: on_device(): lax.all_to_all(outgoing, ('elem', 'span'), split_axis=1, concat_axis=1, t...]
    unnamed x20 -> x36, local copies, waits for them, and re-layouts: 0.05 us -> 4.65 us
  transfers between devices with their start and end apart: 6 -> 4, of which waited for: 3 -> 2; matrix products, arithmetic and copies ran while one was open for 13% -> 0% of each run, Pallas kernels for 0% -> 0%
where the time goes in v1:
time: 79.7 us; the launch traced here: 80.1 us
  starting transfers between devices  36.4 us (46%)
  Pallas kernels  19.7 us (25%)
  local copies, waits for them, and re-layouts  16 us (20%)
  other arithmetic  4.92 us (6%)
  waiting for transfers between devices  2.78 us (3%)
    ppermute x4, starting transfers between devices, shift(): lax.ppermute(value, axis, [(i, (i + step) % count) for i in range(count)])  36.4 us
    pallas_call x1, Pallas kernels, run_net(): pl.pallas_call(net_kernel, out_shape=jax.ShapeDtypeStruct((rows, feat), j...  19.7 us
    unnamed x36, local copies, waits for them, and re-layouts  4.65 us
    scatter x1, local copies, waits for them, and re-layouts, on_device(): return owned.at[edge_local.reshape(-1)].set(merged)  3.86 us
    ppermute x4, waiting for transfers between devices, shift(): lax.ppermute(value, axis, [(i, (i + step) % count) for i in range(count)])  2.78 us
    transpose x4, other arithmetic, band(): flat = jnp.swapaxes(weight, -3, -2).reshape(lead + (out, taps * inn))  2.57 us
    gather x1, local copies, waits for them, and re-layouts, on_device(): edge_rows = owned[edge_local]  2.54 us
    transpose x5, local copies, waits for them, and re-layouts, band(): flat = jnp.swapaxes(weight, -3, -2).reshape(lead + (out, taps * inn))  1.64 us
  transfers between devices with their start and end apart: 4, of which 2 were waited for; matrix products, arithmetic and copies ran while one was open for 0% of the time, Pallas kernels for 0%

profile of v1, /device:TPU:1, one launch (start us, length us, event | category | flops | bytes accessed | tf_op | source)
XLA Modules:
  0.0 80.1 jit_solution(3253838010839898458)
XLA Ops:
  0.0 0.8 multiply_convert_fusion
  0.8 0.8 %multiply_bitcast_fusion.3 = bf16[32,3,32]{2,0,1:T(8,128)(2,1)S(1)} fusion(bf16[3,32,96]{2,1,0:T(8,128)(2,1)} %param.17), kind=kLoop, calls=%fused_computation.63 | loop fusion | flops 3072 | bytes 12288 | tf_op jit(solution)/shard_map/transpose | solution.py:25
  1.6 0.9 %multiply_bitcast_fusion.2 = bf16[8,32,3,32]{3,1,2,0:T(8,128)(2,1)S(1)} fusion(bf16[8,3,32,32]{3,2,1,0:T(8,128)(2,1)} %param.14), kind=kLoop, calls=%fused_computation.20 | loop fusion | flops 24576 | bytes 98304 | tf_op jit(solution)/shard_map/transpose | solution.py:25
  2.7 0.2 reshape.87
  3.5 0.2 reshape.91
  3.7 0.7 pad_dynamic-update-slice_fusion.5
  4.3 0.8 pad_dynamic-update-slice_fusion.4
  5.1 0.8 pad_dynamic-update-slice_fusion.3
  5.9 0.8 pad_dynamic-update-slice_fusion.2
  6.6 0.7 pad_dynamic-update-slice_fusion.1
  8.3 0.8 multiply_bitcast_fusion
  9.1 1.3 %copy.28 = bf16[8,64,3,64]{1,3,2,0:T(8,128)(2,1)S(1)} copy(bf16[8,64,3,64]{3,1,2,0:T(8,128)(2,1)} %multiply_bitcast_fusion) | data formatting | bytes 393216 | tf_op jit(solution)/shard_map/transpose | solution.py:25
  10.4 0.9 %copy.29 = bf16[8,64,192]{2,1,0:T(8,128)(2,1)} copy(bf16[8,64,192]{1,2,0:T(8,128)(2,1)S(1)} %bitcast.37) | data formatting | bytes 393216 | tf_op jit(solution)/shard_map/reshape | solution.py:25
  11.3 1.2 %fusion.2.wm2 = bf16[8,128,256]{2,1,0:T(8,128)(2,1)S(1)} fusion(bf16[8,64,192]{2,1,0:T(8,128)(2,1)} %copy.29), kind=kLoop, calls=%fused_computation.6 | loop fusion | flops 2097152 | bytes 720896 | tf_op jit(solution)/shard_map/concatenate | solution.py:30
  13.1 0.8 pad_dynamic-update-slice_fusion
  13.9 0.7 dynamic_slice.3.sizes
  14.6 19.7 %shard_map.100 = bf16[768,1152]{1,0:T(8,128)(2,1)} custom-call(s32[1]{0:T(128)} %dynamic_slice.3.sizes, bf16[768,1152]{1,0:T(8,128)(2,1)S(1)} %copy-done, bf16[192,128]{1,0:T(8,128)(2,1)S(1)} %constant_dynamic-update-slice_fusion.we1, bf16[8,192,256]{2,1,0:T(8,128)(2,1)S(1)} %get-tuple-element.14.we2, bf16[192,160]{1,0:T(8,128)(2,1)S(1)} %fusion.16.wm1, ...), custom_call_target="tpu_custom_call" | custom-call | tf_op jit(solution)/shard_map/pallas_call | solution.py:139
  34.4 2.5 %gather_fusion = bf16[64,1152]{1,0:T(8,128)(2,1)S(1)} fusion(bf16[768,1152]{1,0:T(8,128)(2,1)} %shard_map.100, s32[1024]{0:T(1024)S(1)} %pad_clamp_fusion), kind=kCustom, calls=%fused_computation | custom fusion | bytes 295168 | tf_op jit(solution)/shard_map/gather | solution.py:187
  36.9 2.1 %collective-permute-start = (bf16[16,1152]{1,0:T(8,128)(2,1)S(1)}, bf16[16,1152]{1,0:T(8,128)(2,1)S(1)}, u32[]{:S(2)}, u32[]{:S(2)}) collective-permute-start(bf16[16,1152]{1,0:T(8,128)(2,1)S(1)} %get-tuple-element.5), channel_id=1, source_target_pairs={{0,4},{4,8},{8,12},{12,16},{16,20},{20,24},{24,28},{28,0},{1,5},{5... | collective-permute-start | bytes 110600 | tf_op jit(solution)/shard_map/ppermute | solution.py:178
  39.0 33.8 %collective-permute-start.1 = (bf16[16,1152]{1,0:T(8,128)(2,1)S(1)}, bf16[16,1152]{1,0:T(8,128)(2,1)S(1)}, u32[]{:S(2)}, u32[]{:S(2)}) collective-permute-start(bf16[16,1152]{1,0:T(8,128)(2,1)S(1)} %get-tuple-element.8), channel_id=1, source_target_pairs={{0,28},{4,0},{8,4},{12,8},{16,12},{20,16},{24,20},{28,24},{1,29},{... | collective-permute-start | bytes 110600 | tf_op jit(solution)/shard_map/ppermute | solution.py:178
  72.8 0.5 collective-permute-start.3
  73.4 0.7 collective-permute-done
  74.1 2.1 %collective-permute-done.3 = bf16[16,1152]{1,0:T(8,128)(2,1)S(1)} collective-permute-done((bf16[16,1152]{1,0:T(8,128)(2,1)S(1)}, bf16[16,1152]{1,0:T(8,128)(2,1)S(1)}, u32[]{:S(2)}, u32[]{:S(2)}) %collective-permute-start.3) | collective-permute-done | bytes 36896 | tf_op jit(solution)/shard_map/ppermute | solution.py:178
  76.2 3.9 %scatter_fusion = bf16[768,1152]{1,0:T(8,128)(2,1)} fusion(bf16[768,1152]{1,0:T(8,128)(2,1)} %shard_map.100, s32[64]{0:T(128)S(1)} %fusion.24, bf16[64,1152]{1,0:T(8,128)(2,1)S(1)} %bitcast.39), kind=kCustom, calls=%fused_computation.1 | custom fusion | bytes 442624 | tf_op jit(solution)/shard_map/scatter | solution.py:195
  (61 shorter events, 2.4 us)
Async XLA Ops:
  0.0 3.3 %copy-start.2 = (bf16[8,3,32,32]{3,2,1,0:T(8,128)(2,1)S(1)}, bf16[8,3,32,32]{3,2,1,0:T(8,128)(2,1)}, u32[]{:S(2)}) copy-start(bf16[8,3,32,32]{3,2,1,0:T(8,128)(2,1)} %param.18) | copy-start | bytes 147460
  2.7 4.6 %copy-start.4 = (bf16[3,16,32]{2,1,0:T(8,128)(2,1)S(1)}, bf16[3,16,32]{2,1,0:T(8,128)(2,1)}, u32[]{:S(2)}) copy-start(bf16[3,16,32]{2,1,0:T(8,128)(2,1)} %param.19) | copy-start | bytes 9220
  2.7 5.0 %copy-start.5 = (bf16[3,32,16]{1,2,0:T(8,128)(2,1)S(1)}, bf16[3,32,16]{1,2,0:T(8,128)(2,1)}, u32[]{:S(2)}) copy-start(bf16[3,32,16]{1,2,0:T(8,128)(2,1)} %param.13) | copy-start | bytes 9220
  2.9 5.4 %copy-start.1 = (bf16[8,3,64,64]{3,2,1,0:T(8,128)(2,1)S(1)}, bf16[8,3,64,64]{3,2,1,0:T(8,128)(2,1)}, u32[]{:S(2)}) copy-start(bf16[8,3,64,64]{3,2,1,0:T(8,128)(2,1)} %param.16) | copy-start | bytes 589828
  6.6 5.9 %copy-start.3 = (bf16[3,64,32]{1,2,0:T(8,128)(2,1)S(1)}, bf16[3,64,32]{1,2,0:T(8,128)(2,1)}, u32[]{:S(2)}) copy-start(bf16[3,64,32]{1,2,0:T(8,128)(2,1)} %param.15) | copy-start | bytes 36868
  7.8 5.2 %copy-start.6 = (s32[1,4,16]{2,1,0:T(4,128)S(1)}, s32[1,4,16]{2,1,0:T(4,128)}, u32[]{:S(2)}) copy-start(s32[1,4,16]{2,1,0:T(4,128)} %param.12) | copy-start | bytes 772
  8.3 5.6 %copy-start.7 = (s32[32]{0:T(128)S(1)}, s32[32]{0:T(128)}, u32[]{:S(2)}) copy-start(s32[32]{0:T(128)} %param.11) | copy-start | bytes 388
  9.1 5.5 %copy-start = (bf16[768,1152]{1,0:T(8,128)(2,1)S(1)}, bf16[768,1152]{1,0:T(8,128)(2,1)}, u32[]{:S(2)}) copy-start(bf16[768,1152]{1,0:T(8,128)(2,1)} %x_ref.1) | copy-start | bytes 5308420
  36.9 37.2 %collective-permute-start = (bf16[16,1152]{1,0:T(8,128)(2,1)S(1)}, bf16[16,1152]{1,0:T(8,128)(2,1)S(1)}, u32[]{:S(2)}, u32[]{:S(2)}) collective-permute-start(bf16[16,1152]{1,0:T(8,128)(2,1)S(1)} %get-tuple-element.5), channel_id=1, source_target_pairs={{0,4},{4,8},{8,12},{12,16},{16,20},{20,24},{24,28},{28,0},{1,5},{5... | collective-permute-start | bytes 110600 | tf_op jit(solution)/shard_map/ppermute | solution.py:178
  39.0 35.1 %collective-permute-start.1 = (bf16[16,1152]{1,0:T(8,128)(2,1)S(1)}, bf16[16,1152]{1,0:T(8,128)(2,1)S(1)}, u32[]{:S(2)}, u32[]{:S(2)}) collective-permute-start(bf16[16,1152]{1,0:T(8,128)(2,1)S(1)} %get-tuple-element.8), channel_id=1, source_target_pairs={{0,28},{4,0},{8,4},{12,8},{16,12},{20,16},{24,20},{28,24},{1,29},{... | collective-permute-start | bytes 110600 | tf_op jit(solution)/shard_map/ppermute | solution.py:178
  72.8 1.3 %collective-permute-start.2 = (bf16[16,1152]{1,0:T(8,128)(2,1)S(1)}, bf16[16,1152]{1,0:T(8,128)(2,1)S(1)}, u32[]{:S(2)}, u32[]{:S(2)}) collective-permute-start(bf16[16,1152]{1,0:T(8,128)(2,1)S(1)} %get-tuple-element.7), channel_id=1, source_target_pairs={{0,1},{1,2},{2,3},{3,0},{4,5},{5,6},{6,7},{7,4},{8,9},{9,10},{10,1... | collective-permute-start | bytes 110600 | tf_op jit(solution)/shard_map/ppermute | solution.py:178
  72.8 3.4 %collective-permute-start.3 = (bf16[16,1152]{1,0:T(8,128)(2,1)S(1)}, bf16[16,1152]{1,0:T(8,128)(2,1)S(1)}, u32[]{:S(2)}, u32[]{:S(2)}) collective-permute-start(bf16[16,1152]{1,0:T(8,128)(2,1)S(1)} %get-tuple-element.6), channel_id=1, source_target_pairs={{0,3},{1,0},{2,1},{3,2},{4,7},{5,4},{6,5},{7,6},{8,11},{9,8},{10,9... | collective-permute-start | bytes 110600 | tf_op jit(solution)/shard_map/ppermute | solution.py:178

commit v2 on v1

v2 whole, which is shorter than its diff:
```python
import functools

import jax
import jax.numpy as jnp
from jax import lax
from jax.experimental import pallas as pl
from jax.experimental.pallas import tpu as pltpu
from jax.sharding import PartitionSpec as P

LEV = 72
HALF = LEV // 2
F_IN = 16
F_OUT = 16
C1 = 32
C2 = 64
DEPTH = 8
FEAT = F_IN * LEV
LANES = 128
NB = 256


def fill_band(dst, taps, levels, layer=None):
    out, inn = taps[0].shape
    lanes = -(-(levels + 2) * inn // LANES) * LANES
    flat = jnp.concatenate(taps + [jnp.zeros((out, lanes - 3 * inn), jnp.float32)], axis=1)
    for d in range(levels):
        moved = flat if d == 0 else pltpu.roll(flat, d * inn, 1)
        moved = moved[:, : (levels + 2) * inn].astype(jnp.bfloat16)
        if layer is None:
            dst[d * out : (d + 1) * out, :] = moved
        else:
            dst[layer, d * out : (d + 1) * out, :] = moved


def taps_of(ref, scale, layer=None, lo=None, hi=None):
    found = []
    for t in range(3):
        tap = (ref[t] if layer is None else ref[layer, t]).astype(jnp.float32) * scale
        found.append(tap[:, lo:hi])
    return found


def build_bands(raw, bands):
    e1, e2, m1, m2, d1, d2, wo = raw
    be1, be2, bm1, bm2, bdm, bds, bd2, bo = bands
    fill_band(be1, taps_of(e1, 0.5), 6)
    fill_band(bm1, taps_of(m1, 0.5), 3)
    fill_band(bds, taps_of(d1, 0.5, lo=C2, hi=C2 + C1), 4)
    fill_band(bo, taps_of(wo, 1.0), 6)
    w = taps_of(d1, 0.5, lo=0, hi=C2)
    zero = jnp.zeros_like(w[0])
    first, both, late, last = w[0], w[1] + w[2], w[0] + w[1], w[2]
    rows = [
        [first, both, zero, zero],
        [zero, late, last, zero],
        [zero, first, both, zero],
        [zero, zero, late, last],
    ]
    for d, row in enumerate(rows):
        bdm[d * C1 : (d + 1) * C1, :] = jnp.concatenate(row, axis=1).astype(jnp.bfloat16)

    def layer_bands(layer, carry):
        fill_band(be2, taps_of(e2, 0.5, layer), 6, layer)
        fill_band(bm2, taps_of(m2, 0.5, layer), 2, layer)
        fill_band(bd2, taps_of(d2, 0.5, layer), 6, layer)
        return carry

    lax.fori_loop(0, DEPTH, layer_bands, 0)


BAND_SHAPES = (
    (6 * C1, 8 * F_IN),
    (DEPTH, 6 * C1, 8 * C1),
    (3 * C2, 5 * C1),
    (DEPTH, 2 * C2, 4 * C2),
    (4 * C1, 4 * C2),
    (4 * C1, 6 * C1),
    (DEPTH, 6 * C1, 8 * C1),
    (6 * F_OUT, 8 * C1),
)


def half_silu(acc):
    return acc + acc * jnp.tanh(acc)


def dot(a, b):
    return jnp.dot(a, b, preferred_element_type=jnp.float32)


def stack_layers(src, dst, w_ref, channels, per, blocks, width):
    def one(layer, source, target):
        w = w_ref[layer]
        for j in range(blocks):
            lo = j * per * channels
            acc = dot(w, source[lo : lo + width, :])
            mid = slice(lo + channels, lo + channels + per * channels)
            target[mid, :] = source[mid, :] + half_silu(acc).astype(jnp.bfloat16)

    def pair(step, carry):
        one(2 * step, src, dst)
        one(2 * step + 1, dst, src)
        return carry

    lax.fori_loop(0, DEPTH // 2, pair, 0)


def clear(scratch):
    for ref in scratch[1:]:
        ref[...] = jnp.zeros_like(ref)


def block_net(live, x_ref, bands, y_ref, scratch):
    we1, we2, wm1, wm2, wdm, wds, wd2, wo = bands
    wide, xin, ha, hb, hc, pool, ma, mb = scratch
    for part in range(NB // LANES):
        here = slice(part * LANES, (part + 1) * LANES)
        wide[part] = x_ref[here, :].astype(jnp.float32).T
        for l in range(LEV):
            xin[F_IN * (l + 1) : F_IN * (l + 2), here] = wide[
                part, pl.ds(l, F_IN, stride=LEV), :
            ].astype(jnp.bfloat16)
    w = we1[...]
    for j in range(12):
        acc = dot(w, xin[96 * j : 96 * j + 128, :])
        ha[192 * j + 32 : 192 * j + 224, :] = half_silu(acc).astype(jnp.bfloat16)
    stack_layers(ha, hb, we2, C1, 6, 12, 256)
    for l in range(HALF):
        even = ha[64 * l + 32 : 64 * l + 64, :].astype(jnp.float32)
        odd = ha[64 * l + 64 : 64 * l + 96, :].astype(jnp.float32)
        pool[32 * l + 32 : 32 * l + 64, :] = (0.5 * (even + odd)).astype(jnp.bfloat16)
    w = wm1[...]
    for j in range(12):
        acc = dot(w, pool[96 * j : 96 * j + 160, :])
        ma[192 * j + 64 : 192 * j + 256, :] = half_silu(acc).astype(jnp.bfloat16)
    stack_layers(ma, mb, wm2, C2, 2, 18, 256)
    w = wdm[...]
    ws = wds[...]
    for j in range(18):
        acc = dot(w, ma[128 * j : 128 * j + 256, :]) + dot(ws, ha[128 * j : 128 * j + 192, :])
        hc[128 * j + 32 : 128 * j + 160, :] = half_silu(acc).astype(jnp.bfloat16)
    stack_layers(hc, hb, wd2, C1, 6, 12, 256)
    w = wo[...]
    for j in range(12):
        acc = dot(w, hc[192 * j : 192 * j + 256, :])
        for d in range(6):
            for part in range(NB // LANES):
                wide[part, pl.ds(6 * j + d, F_OUT, stride=LEV), :] = acc[
                    F_OUT * d : F_OUT * (d + 1), part * LANES : (part + 1) * LANES
                ]
    for part in range(NB // LANES):
        result = wide[part].T
        rows = lax.broadcasted_iota(jnp.int32, result.shape, 0) + part * LANES
        y_ref[part * LANES : (part + 1) * LANES, :] = jnp.where(
            rows < live, result, 0.0
        ).astype(jnp.bfloat16)


def first_kernel(sizes, x_ref, place, *refs):
    raw, bands, y_ref, edge_ref, scratch = refs[:7], refs[7:15], refs[15], refs[16], refs[17:]
    clear(scratch)
    build_bands(raw, bands)
    block_net(sizes[0], x_ref, bands, y_ref, scratch)
    lanes = lax.broadcasted_iota(jnp.int32, (place.shape[0], NB), 1)
    pick = jnp.where(lanes == place[...], 1.0, 0.0).astype(jnp.bfloat16)
    edge_ref[...] = dot(pick, y_ref[...]).astype(jnp.bfloat16)


def rest_kernel(sizes, x_ref, last_ref, *refs):
    bands, y_ref, scratch = refs[:8], refs[8], refs[9:]
    step = pl.program_id(0)
    live = sizes[step]

    @pl.when(step == 0)
    def _():
        clear(scratch)

    @pl.when(live <= 0)
    def _():
        y_ref[...] = jnp.zeros_like(y_ref)

    @pl.when(jnp.logical_and(live > 0, step == 0))
    def _():
        scratch[8][...] = x_ref[...]

    @pl.when(jnp.logical_and(live > 0, step > 0))
    def _():
        scratch[8][...] = last_ref[...]

    @pl.when(live > 0)
    def _():
        block_net(live, scratch[8], bands, y_ref, scratch[:8])


def final_kernel(sizes, y0, rest, back, place, edges, west, east, south, north, out):
    count, moved, offset = sizes[0], sizes[1], sizes[2]
    across = jnp.concatenate([r[...].astype(jnp.float32) for r in (west, east, south, north)], axis=0)
    merged = (0.5 * (edges[...].astype(jnp.float32) + across)).astype(jnp.bfloat16)
    rows = lax.broadcasted_iota(jnp.int32, (NB, merged.shape[0]), 0)
    pick = jnp.where(rows == place[...], 1.0, 0.0)
    hit = jnp.sum(pick, axis=1, keepdims=True) > 0.0
    chosen = dot(pick.astype(jnp.bfloat16), merged)
    out[0:NB, :] = jnp.where(hit, chosen, y0[...].astype(jnp.float32)).astype(jnp.bfloat16)
    at = lax.broadcasted_iota(jnp.int32, (NB, 1), 0)
    out[NB : 2 * NB, :] = jnp.where(
        at + NB < count, rest[0:NB, :].astype(jnp.float32), 0.0
    ).astype(jnp.bfloat16)

    @pl.when(moved == 0)
    def _():
        out[2 * NB : 3 * NB, :] = rest[NB : 2 * NB, :]

    @pl.when(moved > 0)
    def _():
        turned = pltpu.roll(back[...].astype(jnp.float32), lax.rem(NB - offset, NB), 0)
        out[2 * NB : 3 * NB, :] = jnp.where(at + 2 * NB < count, turned, 0.0).astype(jnp.bfloat16)


def whole_spec(shape):
    return pl.BlockSpec(shape, lambda *_: (0,) * len(shape))


def net_scratch():
    outer = (LEV + 2) * C1
    inner = (HALF + 2) * C2
    return [
        pltpu.VMEM((NB // LANES, FEAT, LANES), jnp.float32),
        pltpu.VMEM(((LEV + 2) * F_IN, NB), jnp.bfloat16),
        pltpu.VMEM((outer, NB), jnp.bfloat16),
        pltpu.VMEM((outer, NB), jnp.bfloat16),
        pltpu.VMEM((outer, NB), jnp.bfloat16),
        pltpu.VMEM(((HALF + 2) * C1, NB), jnp.bfloat16),
        pltpu.VMEM((inner, NB), jnp.bfloat16),
        pltpu.VMEM((inner, NB), jnp.bfloat16),
    ]


def bf16(*shape):
    return jax.ShapeDtypeStruct(shape, jnp.bfloat16)


def call(kernel, out_shape, grid, in_specs, out_specs, scratch, flops, operands):
    return pl.pallas_call(
        kernel,
        out_shape=out_shape,
        grid_spec=pltpu.PrefetchScalarGridSpec(
            num_scalar_prefetch=1,
            grid=grid,
            in_specs=in_specs,
            out_specs=out_specs,
            scratch_shapes=scratch,
        ),
        compiler_params=pltpu.CompilerParams(vmem_limit_bytes=48 * 1024 * 1024),
        cost_estimate=pl.CostEstimate(flops=flops, bytes_accessed=4000000, transcendentals=0),
    )(*operands)


def run_first(columns, size, place, weights):
    entries = place.shape[0]
    block = whole_spec((NB, FEAT))
    shapes = BAND_SHAPES + ((NB, FEAT), (entries, FEAT))
    found = call(
        first_kernel,
        [bf16(*shape) for shape in shapes],
        (1,),
        [block, whole_spec(place.shape)] + [whole_spec(w.shape) for w in weights],
        [whole_spec(shape) for shape in shapes],
        net_scratch(),
        15 * 10**9,
        (size, columns, place) + tuple(weights),
    )
    return found[:8], found[8], found[9]


def run_rest(second, columns, sizes, bands):
    block = pl.BlockSpec((NB, FEAT), lambda g, s: (0, 0))
    last = pl.BlockSpec((NB, FEAT), lambda g, s: (2, 0))
    return call(
        rest_kernel,
        bf16(2 * NB, FEAT),
        (2,),
        [block, last] + [whole_spec(b.shape) for b in bands],
        pl.BlockSpec((NB, FEAT), lambda g, s: (g, 0)),
        net_scratch() + [pltpu.VMEM((NB, FEAT), jnp.bfloat16)],
        20 * 10**9,
        (sizes, second, columns) + tuple(bands),
    )


def run_final(sizes, operands, rows):
    return call(
        final_kernel,
        bf16(rows, FEAT),
        (1,),
        [whole_spec(v.shape) for v in operands],
        whole_spec((rows, FEAT)),
        [],
        10**8,
        (sizes,) + tuple(operands),
    )


def shift(value, axis, step):
    count = lax.axis_size(axis)
    return lax.ppermute(value, axis, [(i, (i + step) % count) for i in range(count)])


def on_device(column_state, counts, edge_index, *weights):
    device_index = lax.axis_index(("elem", "span"))
    span = lax.axis_size("span")
    own = counts[device_index]
    other = counts[device_index ^ 1]
    fits = own + other <= 4 * NB
    gives = jnp.logical_and(fits, own > 2 * NB)
    takes = jnp.logical_and(fits, other > 2 * NB)
    offset_out = jnp.maximum(other, NB) - NB
    offset_in = jnp.maximum(own, NB) - NB
    swap = [(i, i ^ 1) for i in range(span)]

    start = jnp.clip(2 * NB - offset_out, 0, column_state.shape[0] - NB)
    slab = lax.dynamic_slice_in_dim(column_state, start, NB, axis=0)
    arrived = lax.ppermute(slab, "span", swap)

    edge_flat = edge_index.reshape(-1)
    bands, y0, edge_rows = run_first(column_state, own[None], edge_flat[:, None], weights)
    side = edge_rows.reshape(4, -1, FEAT)
    from_west = shift(side[1], "elem", 1)
    from_east = shift(side[0], "elem", -1)
    from_south = shift(side[3], "span", 1)
    from_north = shift(side[2], "span", -1)

    at = jnp.arange(NB, dtype=jnp.int32)[:, None]
    second = jnp.where(
        jnp.logical_and(takes, at >= offset_in), arrived, column_state[NB : 2 * NB]
    )
    live_second = jnp.where(takes, offset_in + other - 2 * NB, jnp.minimum(own - NB, NB))
    live_last = jnp.where(gives, 0, own - 2 * NB)
    rest = run_rest(second, column_state, jnp.stack([live_second, live_last]), bands)
    back = lax.ppermute(rest[:NB], "span", swap)
    sizes = jnp.stack([own, gives.astype(jnp.int32), jnp.clip(offset_out, 0, NB)])
    return run_final(
        sizes,
        (y0, rest, back, edge_flat[None, :], edge_rows, from_west, from_east, from_south, from_north),
        column_state.shape[0],
    )


def solution(mesh):
    return jax.shard_map(
        on_device,
        mesh=mesh,
        in_specs=(P(("elem", "span"), None), P(), P(("elem", "span"), None, None)) + (P(),) * 7,
        out_specs=P(("elem", "span"), None),
        check_vma=False,
    )
```

time: 79.7 us -> 70.9 us (0.89); the launches traced: 80.1 us -> 70.5 us
  starting transfers between devices: 36.4 us -> 20.5 us
  between operations: 0.28 us -> 5.54 us
  local copies, waits for them, and re-layouts: 16 us -> 20.9 us
  other arithmetic: 4.92 us -> 2.09 us
  Pallas kernels: 19.7 us -> 18.8 us
    ppermute x4, starting transfers between devices: 36.4 us -> 19.9 us  [shift(): lax.ppermute(value, axis, [(i, (i + step) % count) for i in range(count)])]
    unnamed x36 -> x56, local copies, waits for them, and re-layouts: 4.65 us -> 17.4 us
    scatter x1 -> x0, local copies, waits for them, and re-layouts: 3.86 us -> none  [on_device(): return owned.at[edge_local.reshape(-1)].set(merged)]
    transpose x4 -> x0, other arithmetic: 2.57 us -> none  [band(): flat = jnp.swapaxes(weight, -3, -2).reshape(lead + (out, taps * inn))]
    gather x1 -> x0, local copies, waits for them, and re-layouts: 2.54 us -> none  [on_device(): edge_rows = owned[edge_local]]
    transpose x5 -> x0, local copies, waits for them, and re-layouts: 1.64 us -> none  [band(): flat = jnp.swapaxes(weight, -3, -2).reshape(lead + (out, taps * inn))]
    reshape x7 -> x0, local copies, waits for them, and re-layouts: 1.55 us -> none  [band(): flat = jnp.swapaxes(weight, -3, -2).reshape(lead + (out, taps * inn))]
    concatenate x4 -> x0, other arithmetic: 1.49 us -> none  [the longest x3 1.39 us: band(): return jnp.concatenate(rows, axis=-2)]
  transfers between devices with their start and end apart: 4 -> 6, of which waited for: 2 -> 2; matrix products, arithmetic and copies ran while one was open for 0% -> 5% of each run, Pallas kernels for 0% -> 22%
where the time goes in v2:
time: 70.9 us; the launch traced here: 70.5 us
  local copies, waits for them, and re-layouts  20.9 us (29%)
  starting transfers between devices  20.5 us (29%)
  Pallas kernels  18.8 us (27%)
  between operations  5.54 us (8%)
  waiting for transfers between devices  2.59 us (4%)
  other arithmetic  2.09 us (3%)
    ppermute x4, starting transfers between devices, shift(): lax.ppermute(value, axis, [(i, (i + step) % count) for i in range(count)])  19.9 us
    pallas_call x3, Pallas kernels, call(): pl.pallas_call(kernel, out_shape=out_shape, grid_spec=pltpu.PrefetchScala...  18.8 us
    unnamed x56, local copies, waits for them, and re-layouts  17.4 us
    ppermute x4, waiting for transfers between devices, shift(): lax.ppermute(value, axis, [(i, (i + step) % count) for i in range(count)])  2.58 us
  transfers between devices with their start and end apart: 6, of which 2 were waited for; matrix products, arithmetic and copies ran while one was open for 5% of the time, Pallas kernels for 22%

profile of v2, /device:TPU:1, one launch (start us, length us, event | category | flops | bytes accessed | tf_op | source)
XLA Modules:
  0.0 70.5 jit_solution(17989195762374825569)
XLA Ops:
  0.0 1.3 %fusion.1 = (s32[1]{0:T(128)}, s32[1]{0:T(128)}) fusion(s32[32]{0:T(128)} %param.11, s32[]{:T(128)S(6)} %select_n.19, s32[]{:T(128)S(6)} %select_n.20), kind=kLoop, calls=%fused_computation.6 | loop fusion | bytes 24 | tf_op jit(solution)/shard_map/dynamic_slice | solution.py:311
  1.9 1.2 %constant_dynamic-slice_fusion = bf16[256,1152]{1,0:T(8,128)(2,1)S(1)} fusion(bf16[768,1152]{1,0:T(8,128)(2,1)} %last_ref.1, s32[]{:T(128)S(6)} %min.12), kind=kLoop, calls=%fused_computation.4 | loop fusion | bytes 1179652 | tf_op jit(solution)/shard_map/dynamic_slice | solution.py:321
  3.2 0.8 %broadcast_in_dim_reshape.8.place = s32[64,1]{1,0:T(8,128)S(1)} reshape(s32[1,4,16]{2,1,0:T(4,128)} %param.12) | data formatting | bytes 512 | tf_op jit(solution)/shard_map/broadcast_in_dim;reshape | solution.py:325
  4.0 0.8 %copy.12.refs_0_ = bf16[3,32,16]{2,1,0:T(8,128)(2,1)S(1)} copy(bf16[3,32,16]{1,2,0:T(8,128)(2,1)} %param.13) | data formatting | bytes 6144 | tf_op args[3]
  4.8 0.8 %copy.13.refs_2_ = bf16[3,64,32]{2,1,0:T(8,128)(2,1)S(1)} copy(bf16[3,64,32]{1,2,0:T(8,128)(2,1)} %param.15) | data formatting | bytes 24576 | tf_op args[5]
  5.7 1.5 %copy-done = bf16[768,1152]{1,0:T(8,128)(2,1)S(1)} copy-done((bf16[768,1152]{1,0:T(8,128)(2,1)S(1)}, bf16[768,1152]{1,0:T(8,128)(2,1)}, u32[]{:S(2)}) %copy-start) | copy-done | bytes 1769496
  7.1 1.0 %copy-done.5 = bf16[8,3,64,64]{3,2,1,0:T(8,128)(2,1)S(1)} copy-done((bf16[8,3,64,64]{3,2,1,0:T(8,128)(2,1)S(1)}, bf16[8,3,64,64]{3,2,1,0:T(8,128)(2,1)}, u32[]{:S(2)}) %copy-start.5) | copy-done | bytes 196632
  8.1 0.9 %copy-done.6 = bf16[8,3,32,32]{3,2,1,0:T(8,128)(2,1)S(1)} copy-done((bf16[8,3,32,32]{3,2,1,0:T(8,128)(2,1)S(1)}, bf16[8,3,32,32]{3,2,1,0:T(8,128)(2,1)}, u32[]{:S(2)}) %copy-start.6) | copy-done | bytes 49176
  9.0 0.9 %copy-done.7 = bf16[8,3,32,32]{3,2,1,0:T(8,128)(2,1)S(1)} copy-done((bf16[8,3,32,32]{3,2,1,0:T(8,128)(2,1)S(1)}, bf16[8,3,32,32]{3,2,1,0:T(8,128)(2,1)}, u32[]{:S(2)}) %copy-start.7) | copy-done | bytes 49176
  10.0 0.7 %copy-done.8 = bf16[3,32,96]{2,1,0:T(8,128)(2,1)S(1)} copy-done((bf16[3,32,96]{2,1,0:T(8,128)(2,1)S(1)}, bf16[3,32,96]{2,1,0:T(8,128)(2,1)}, u32[]{:S(2)}) %copy-start.8) | copy-done | bytes 18456
  11.4 15.5 %shard_map.100 = (bf16[192,128]{1,0:T(8,128)(2,1)S(1)}, bf16[8,192,256]{2,1,0:T(8,128)(2,1)S(1)}, bf16[192,160]{1,0:T(8,128)(2,1)S(1)}, bf16[8,128,256]{2,1,0:T(...) custom-call(s32[1]{0:T(128)} %get-tuple-element.29.sizes, ...), custom_call_target="tpu_custom_call" | custom-call | flops 15000000512 | bytes 4000000 | tf_op jit(solution)/shard_map/pallas_call | solution.py:243
  27.6 0.9 %copy-done.10 = bf16[8,192,256]{2,1,0:T(8,128)(2,1)} copy-done((bf16[8,192,256]{2,1,0:T(8,128)(2,1)}, bf16[8,192,256]{2,1,0:T(8,128)(2,1)S(1)}, u32[]{:S(2)}) %copy-start.10) | copy-done | bytes 786456
  28.5 0.9 %copy-done.12 = bf16[8,192,256]{2,1,0:T(8,128)(2,1)} copy-done((bf16[8,192,256]{2,1,0:T(8,128)(2,1)}, bf16[8,192,256]{2,1,0:T(8,128)(2,1)S(1)}, u32[]{:S(2)}) %copy-start.12) | copy-done | bytes 786456
  29.4 0.8 %copy-done.14 = bf16[8,128,256]{2,1,0:T(8,128)(2,1)} copy-done((bf16[8,128,256]{2,1,0:T(8,128)(2,1)}, bf16[8,128,256]{2,1,0:T(8,128)(2,1)S(1)}, u32[]{:S(2)}) %copy-start.14) | copy-done | bytes 524312
  38.3 1.3 %slice_select_fusion.x_ref = bf16[256,1152]{1,0:T(8,128)(2,1)S(1)} fusion(bf16[256,1152]{1,0:T(8,128)(2,1)} %collective-permute-done, bf16[768,1152]{1,0:T(8,128)(2,1)S(1)} %copy-done.1, pred[256]{0:T(512)(128)(4,1)S(1)} %compare_and_fusion), kind=kLoop, calls=%fused_computation | loop fusion | flops 294912 | bytes 1769728 | tf_op jit(solution)/shard_map/jit(_where)/select_n | solution.py:333
  39.7 1.0 %copy-done.15 = bf16[8,128,256]{2,1,0:T(8,128)(2,1)S(1)} copy-done((bf16[8,128,256]{2,1,0:T(8,128)(2,1)S(1)}, bf16[8,128,256]{2,1,0:T(8,128)(2,1)}, u32[]{:S(2)}) %copy-start.15) | copy-done | bytes 524312
  40.7 0.8 %copy-done.21 = bf16[128,192]{1,0:T(8,128)(2,1)S(1)} copy-done((bf16[128,192]{1,0:T(8,128)(2,1)S(1)}, bf16[128,192]{1,0:T(8,128)(2,1)}, u32[]{:S(2)}) %copy-start.21) | copy-done | bytes 49176
  41.6 0.8 %copy-done.25 = bf16[96,256]{1,0:T(8,128)(2,1)S(1)} copy-done((bf16[96,256]{1,0:T(8,128)(2,1)S(1)}, bf16[96,256]{1,0:T(8,128)(2,1)}, u32[]{:S(2)}) %copy-start.25) | copy-done | bytes 49176
  42.4 1.2 %shard_map.101.rest = bf16[512,1152]{1,0:T(8,128)(2,1)S(1)} custom-call(s32[2]{0:T(128)S(1)} %pad_add_fusion.1.sizes, bf16[256,1152]{1,0:T(8,128)(2,1)S(1)} %slice_select_fusion.x_ref, bf16[768,1152]{1,0:T(8,128)(2,1)S(1)} %copy-done.1, bf16[192,128]{1,0:T(8,128)(2,1)S(1)} %copy-done.23, bf16[8,192,256]{2,1,0:T(8,128)(2,1)S(1)} %copy-done.11, ...), custom_call_target="tpu_custom_call" | custom-call | flops 20000000000 | bytes 4000000 | tf_op jit(solution)/shard_map/pallas_call | solution.py:243
  44.2 14.9 %collective-permute-start.2 = (bf16[16,1152]{1,0:T(8,128)(2,1)S(1)}, bf16[16,1152]{1,0:T(8,128)(2,1)S(1)}, u32[]{:S(2)}, u32[]{:S(2)}) collective-permute-start(bf16[16,1152]{1,0:T(8,128)(2,1)S(1)} %get-tuple-element.28), channel_id=1, source_target_pairs={{0,4},{4,8},{8,12},{12,16},{16,20},{20,24},{24,28},{28,0},{1,5},{5... | collective-permute-start | bytes 110600 | tf_op jit(solution)/shard_map/ppermute | solution.py:305
  59.0 5.0 %collective-permute-start.4 = (bf16[16,1152]{1,0:T(8,128)(2,1)S(1)}, bf16[16,1152]{1,0:T(8,128)(2,1)S(1)}, u32[]{:S(2)}, u32[]{:S(2)}) collective-permute-start(bf16[16,1152]{1,0:T(8,128)(2,1)S(1)} %get-tuple-element.26), channel_id=1, source_target_pairs={{0,1},{1,2},{2,3},{3,0},{4,5},{5,6},{6,7},{7,4},{8,9},{9,10},{10,1... | collective-permute-start | bytes 110600 | tf_op jit(solution)/shard_map/ppermute | solution.py:305
  65.3 2.1 %collective-permute-done.5.north = bf16[16,1152]{1,0:T(8,128)(2,1)S(1)} collective-permute-done((bf16[16,1152]{1,0:T(8,128)(2,1)S(1)}, bf16[16,1152]{1,0:T(8,128)(2,1)S(1)}, u32[]{:S(2)}, u32[]{:S(2)}) %collective-permute-start.5) | collective-permute-done | bytes 36896 | tf_op jit(solution)/shard_map/ppermute | solution.py:305
  67.4 0.9 %copy-done.4 = bf16[64,1152]{1,0:T(8,128)(2,1)S(1)} copy-done((bf16[64,1152]{1,0:T(8,128)(2,1)S(1)}, bf16[64,1152]{1,0:T(8,128)(2,1)}, u32[]{:S(2)}) %copy-start.4) | copy-done | bytes 147480
  68.3 2.2 %shard_map.102 = bf16[768,1152]{1,0:T(8,128)(2,1)} custom-call(s32[3]{0:T(128)S(1)} %pad_add_fusion.sizes, bf16[256,1152]{1,0:T(8,128)(2,1)S(1)} %get-tuple-element.15.y0, bf16[512,1152]{1,0:T(8,128)(2,1)S(1)} %shard_map.101.rest, bf16[256,1152]{1,0:T(8,128)(2,1)S(1)} %collective-permute-done.1.back, s32[1,64]{1,0:T(1,128)S(1)} %broadcast_in_dim_reshape.7.place, ...), custom_call_target="tpu_custom_call" | custom-call | flops 100000000 | bytes 4000000 | tf_op jit(solution)/shard_map/pallas_call | solution.py:243
  (57 shorter events, 6.7 us)
Async XLA Ops:
  3.1 35.1 %collective-permute-start = (bf16[256,1152]{1,0:T(8,128)(2,1)S(1)}, bf16[256,1152]{1,0:T(8,128)(2,1)}, u32[]{:S(2)}, u32[]{:S(2)}) collective-permute-start(bf16[256,1152]{1,0:T(8,128)(2,1)S(1)} %constant_dynamic-slice_fusion), channel_id=1, source_target_pairs={{0,1},{1,0},{2,3},{3,2},{4,5},{5,4},{6,7},{7,6},{8,9},{9,8},{10,11... | collective-permute-start | bytes 1769480 | tf_op jit(solution)/shard_map/ppermute | solution.py:322
  5.6 1.5 %copy-start = (bf16[768,1152]{1,0:T(8,128)(2,1)S(1)}, bf16[768,1152]{1,0:T(8,128)(2,1)}, u32[]{:S(2)}) copy-start(bf16[768,1152]{1,0:T(8,128)(2,1)} %last_ref.1) | copy-start | bytes 5308420
  7.1 1.0 %copy-start.5 = (bf16[8,3,64,64]{3,2,1,0:T(8,128)(2,1)S(1)}, bf16[8,3,64,64]{3,2,1,0:T(8,128)(2,1)}, u32[]{:S(2)}) copy-start(bf16[8,3,64,64]{3,2,1,0:T(8,128)(2,1)} %refs_3_.1) | copy-start | bytes 589828
  8.1 0.9 %copy-start.6 = (bf16[8,3,32,32]{3,2,1,0:T(8,128)(2,1)S(1)}, bf16[8,3,32,32]{3,2,1,0:T(8,128)(2,1)}, u32[]{:S(2)}) copy-start(bf16[8,3,32,32]{3,2,1,0:T(8,128)(2,1)} %refs_1_.1) | copy-start | bytes 147460
  9.0 0.9 %copy-start.7 = (bf16[8,3,32,32]{3,2,1,0:T(8,128)(2,1)S(1)}, bf16[8,3,32,32]{3,2,1,0:T(8,128)(2,1)}, u32[]{:S(2)}) copy-start(bf16[8,3,32,32]{3,2,1,0:T(8,128)(2,1)} %refs_5_.1) | copy-start | bytes 147460
  11.4 26.8 %copy-start.1 = (bf16[768,1152]{1,0:T(8,128)(2,1)S(1)}, bf16[768,1152]{1,0:T(8,128)(2,1)}, u32[]{:S(2)}) copy-start(bf16[768,1152]{1,0:T(8,128)(2,1)} %last_ref.1) | copy-start | bytes 5308420
  27.6 0.9 %copy-start.10 = (bf16[8,192,256]{2,1,0:T(8,128)(2,1)}, bf16[8,192,256]{2,1,0:T(8,128)(2,1)S(1)}, u32[]{:S(2)}) copy-start(bf16[8,192,256]{2,1,0:T(8,128)(2,1)S(1)} %get-tuple-element.17.refs_1_) | copy-start | bytes 2359300
  28.5 0.9 %copy-start.12 = (bf16[8,192,256]{2,1,0:T(8,128)(2,1)}, bf16[8,192,256]{2,1,0:T(8,128)(2,1)S(1)}, u32[]{:S(2)}) copy-start(bf16[8,192,256]{2,1,0:T(8,128)(2,1)S(1)} %get-tuple-element.22.refs_6_) | copy-start | bytes 2359300
  29.4 0.8 %copy-start.14 = (bf16[8,128,256]{2,1,0:T(8,128)(2,1)}, bf16[8,128,256]{2,1,0:T(8,128)(2,1)S(1)}, u32[]{:S(2)}) copy-start(bf16[8,128,256]{2,1,0:T(8,128)(2,1)S(1)} %get-tuple-element.19.refs_3_) | copy-start | bytes 1572868
  38.1 1.5 %copy-start.11 = (bf16[8,192,256]{2,1,0:T(8,128)(2,1)S(1)}, bf16[8,192,256]{2,1,0:T(8,128)(2,1)}, u32[]{:S(2)}) copy-start(bf16[8,192,256]{2,1,0:T(8,128)(2,1)} %copy-done.10) | copy-start | bytes 2359300
  38.1 1.5 %copy-start.13 = (bf16[8,192,256]{2,1,0:T(8,128)(2,1)S(1)}, bf16[8,192,256]{2,1,0:T(8,128)(2,1)}, u32[]{:S(2)}) copy-start(bf16[8,192,256]{2,1,0:T(8,128)(2,1)} %copy-done.12) | copy-start | bytes 2359300
  38.1 1.5 %copy-start.17 = (bf16[192,160]{1,0:T(8,128)(2,1)S(1)}, bf16[192,160]{1,0:T(8,128)(2,1)}, u32[]{:S(2)}) copy-start(bf16[192,160]{1,0:T(8,128)(2,1)} %copy-done.16) | copy-start | bytes 184324
  38.1 1.5 %copy-start.19 = (bf16[128,256]{1,0:T(8,128)(2,1)S(1)}, bf16[128,256]{1,0:T(8,128)(2,1)}, u32[]{:S(2)}) copy-start(bf16[128,256]{1,0:T(8,128)(2,1)} %copy-done.18) | copy-start | bytes 196612
  38.2 1.5 %copy-start.23 = (bf16[192,128]{1,0:T(8,128)(2,1)S(1)}, bf16[192,128]{1,0:T(8,128)(2,1)}, u32[]{:S(2)}) copy-start(bf16[192,128]{1,0:T(8,128)(2,1)} %copy-done.22) | copy-start | bytes 147460
  39.7 1.0 %copy-start.15 = (bf16[8,128,256]{2,1,0:T(8,128)(2,1)S(1)}, bf16[8,128,256]{2,1,0:T(8,128)(2,1)}, u32[]{:S(2)}) copy-start(bf16[8,128,256]{2,1,0:T(8,128)(2,1)} %copy-done.14) | copy-start | bytes 1572868
  40.7 0.8 %copy-start.21 = (bf16[128,192]{1,0:T(8,128)(2,1)S(1)}, bf16[128,192]{1,0:T(8,128)(2,1)}, u32[]{:S(2)}) copy-start(bf16[128,192]{1,0:T(8,128)(2,1)} %copy-done.20) | copy-start | bytes 147460
  42.4 1.8 %copy-start.3 = (bf16[64,1152]{1,0:T(8,128)(2,1)S(1)}, bf16[64,1152]{1,0:T(8,128)(2,1)}, u32[]{:S(2)}) copy-start(bf16[64,1152]{1,0:T(8,128)(2,1)} %copy-done.2) | copy-start | bytes 442372
  42.4 22.4 %copy-start.26 = (s32[1,4,16]{2,1,0:T(4,128)S(1)}, s32[1,4,16]{2,1,0:T(4,128)}, u32[]{:S(2)}) copy-start(s32[1,4,16]{2,1,0:T(4,128)} %param.12) | copy-start | bytes 772
  43.6 23.8 %collective-permute-start.1 = (bf16[256,1152]{1,0:T(8,128)(2,1)S(1)}, bf16[256,1152]{1,0:T(8,128)(2,1)S(1)}, u32[]{:S(2)}, u32[]{:S(2)}) collective-permute-start(bf16[256,1152]{1,0:T(8,128)(2,1)S(1)} %slice.28), channel_id=1, source_target_pairs={{0,1},{1,0},{2,3},{3,2},{4,5},{5,4},{6,7},{7,6},{8,9},{9,8},{10,11... | collective-permute-start | bytes 1769480 | tf_op jit(solution)/shard_map/ppermute | solution.py:339
  44.2 20.7 %collective-permute-start.2 = (bf16[16,1152]{1,0:T(8,128)(2,1)S(1)}, bf16[16,1152]{1,0:T(8,128)(2,1)S(1)}, u32[]{:S(2)}, u32[]{:S(2)}) collective-permute-start(bf16[16,1152]{1,0:T(8,128)(2,1)S(1)} %get-tuple-element.28), channel_id=1, source_target_pairs={{0,4},{4,8},{8,12},{12,16},{16,20},{20,24},{24,28},{28,0},{1,5},{5... | collective-permute-start | bytes 110600 | tf_op jit(solution)/shard_map/ppermute | solution.py:305
  59.0 5.8 %collective-permute-start.3 = (bf16[16,1152]{1,0:T(8,128)(2,1)S(1)}, bf16[16,1152]{1,0:T(8,128)(2,1)S(1)}, u32[]{:S(2)}, u32[]{:S(2)}) collective-permute-start(bf16[16,1152]{1,0:T(8,128)(2,1)S(1)} %get-tuple-element.27), channel_id=1, source_target_pairs={{0,28},{4,0},{8,4},{12,8},{16,12},{20,16},{24,20},{28,24},{1,29},{... | collective-permute-start | bytes 110600 | tf_op jit(solution)/shard_map/ppermute | solution.py:305
  59.0 6.3 %collective-permute-start.4 = (bf16[16,1152]{1,0:T(8,128)(2,1)S(1)}, bf16[16,1152]{1,0:T(8,128)(2,1)S(1)}, u32[]{:S(2)}, u32[]{:S(2)}) collective-permute-start(bf16[16,1152]{1,0:T(8,128)(2,1)S(1)} %get-tuple-element.26), channel_id=1, source_target_pairs={{0,1},{1,2},{2,3},{3,0},{4,5},{5,6},{6,7},{7,4},{8,9},{9,10},{10,1... | collective-permute-start | bytes 110600 | tf_op jit(solution)/shard_map/ppermute | solution.py:305
  64.0 3.4 %collective-permute-start.5 = (bf16[16,1152]{1,0:T(8,128)(2,1)S(1)}, bf16[16,1152]{1,0:T(8,128)(2,1)S(1)}, u32[]{:S(2)}, u32[]{:S(2)}) collective-permute-start(bf16[16,1152]{1,0:T(8,128)(2,1)S(1)} %get-tuple-element.25), channel_id=1, source_target_pairs={{0,3},{1,0},{2,1},{3,2},{4,7},{5,4},{6,5},{7,6},{8,11},{9,8},{10,9... | collective-permute-start | bytes 110600 | tf_op jit(solution)/shard_map/ppermute | solution.py:305
  67.4 0.9 %copy-start.4 = (bf16[64,1152]{1,0:T(8,128)(2,1)S(1)}, bf16[64,1152]{1,0:T(8,128)(2,1)}, u32[]{:S(2)}) copy-start(bf16[64,1152]{1,0:T(8,128)(2,1)} %copy-done.2) | copy-start | bytes 442372
  (9 other events, 6.0 us)

commit v3 on v2

--- a/solution.py
+++ b/solution.py
@@ -157,7 +157,7 @@
 
 
 def first_kernel(sizes, x_ref, place, *refs):
-    raw, bands, y_ref, edge_ref, scratch = refs[:7], refs[7:15], refs[15], refs[16], refs[17:]
+    raw, y_ref, edge_ref, bands, scratch = refs[:7], refs[7], refs[8], refs[9:17], refs[17:]
     clear(scratch)
     build_bands(raw, bands)
     block_net(sizes[0], x_ref, bands, y_ref, scratch)
@@ -167,13 +167,14 @@
 
 
 def rest_kernel(sizes, x_ref, last_ref, *refs):
-    bands, y_ref, scratch = refs[:8], refs[8], refs[9:]
+    raw, y_ref, bands, scratch = refs[:7], refs[7], refs[8:16], refs[16:]
     step = pl.program_id(0)
     live = sizes[step]
 
-    @pl.when(step == 0)
-    def _():
-        clear(scratch)
+    @pl.when(jnp.logical_and(step == 0, jnp.maximum(live, sizes[1]) > 0))
+    def _():
+        clear(scratch[:8])
+        build_bands(raw, bands)
 
     @pl.when(live <= 0)
     def _():
@@ -223,7 +224,7 @@
 def net_scratch():
     outer = (LEV + 2) * C1
     inner = (HALF + 2) * C2
-    return [
+    return [pltpu.VMEM(shape, jnp.bfloat16) for shape in BAND_SHAPES] + [
         pltpu.VMEM((NB // LANES, FEAT, LANES), jnp.float32),
         pltpu.VMEM(((LEV + 2) * F_IN, NB), jnp.bfloat16),
         pltpu.VMEM((outer, NB), jnp.bfloat16),
@@ -250,7 +251,6 @@
             out_specs=out_specs,
             scratch_shapes=scratch,
         ),
-        compiler_params=pltpu.CompilerParams(vmem_limit_bytes=48 * 1024 * 1024),
         cost_estimate=pl.CostEstimate(flops=flops, bytes_accessed=4000000, transcendentals=0),
     )(*operands)
 
@@ -258,8 +258,8 @@
 def run_first(columns, size, place, weights):
     entries = place.shape[0]
     block = whole_spec((NB, FEAT))
-    shapes = BAND_SHAPES + ((NB, FEAT), (entries, FEAT))
-    found = call(
+    shapes = ((NB, FEAT), (entries, FEAT))
+    return call(
         first_kernel,
         [bf16(*shape) for shape in shapes],
         (1,),
@@ -269,21 +269,20 @@
         15 * 10**9,
         (size, columns, place) + tuple(weights),
     )
-    return found[:8], found[8], found[9]
-
-
-def run_rest(second, columns, sizes, bands):
+
+
+def run_rest(second, columns, sizes, weights):
     block = pl.BlockSpec((NB, FEAT), lambda g, s: (0, 0))
     last = pl.BlockSpec((NB, FEAT), lambda g, s: (2, 0))
     return call(
         rest_kernel,
         bf16(2 * NB, FEAT),
         (2,),
-        [block, last] + [whole_spec(b.shape) for b in bands],
+        [block, last] + [whole_spec(w.shape) for w in weights],
         pl.BlockSpec((NB, FEAT), lambda g, s: (g, 0)),
         net_scratch() + [pltpu.VMEM((NB, FEAT), jnp.bfloat16)],
         20 * 10**9,
-        (sizes, second, columns) + tuple(bands),
+        (sizes, second, columns) + tuple(weights),
     )
 
 
@@ -322,7 +321,7 @@
     arrived = lax.ppermute(slab, "span", swap)
 
     edge_flat = edge_index.reshape(-1)
-    bands, y0, edge_rows = run_first(column_state, own[None], edge_flat[:, None], weights)
+    y0, edge_rows = run_first(column_state, own[None], edge_flat[:, None], weights)
     side = edge_rows.reshape(4, -1, FEAT)
     from_west = shift(side[1], "elem", 1)
     from_east = shift(side[0], "elem", -1)
@@ -335,7 +334,7 @@
     )
     live_second = jnp.where(takes, offset_in + other - 2 * NB, jnp.minimum(own - NB, NB))
     live_last = jnp.where(gives, 0, own - 2 * NB)
-    rest = run_rest(second, column_state, jnp.stack([live_second, live_last]), bands)
+    rest = run_rest(second, column_state, jnp.stack([live_second, live_last]), weights)
     back = lax.ppermute(rest[:NB], "span", swap)
     sizes = jnp.stack([own, gives.astype(jnp.int32), jnp.clip(offset_out, 0, NB)])
     return run_final(

time: 70.9 us -> 68.2 us (0.962)
  Pallas kernels: 18.8 us -> 39.3 us
  starting transfers between devices: 20.5 us -> 4.67 us
  local copies, waits for them, and re-layouts: 20.9 us -> 10.1 us
  other arithmetic: 2.09 us -> 3.86 us
  waiting for transfers between devices: 2.59 us -> 3.45 us
    pallas_call x3, Pallas kernels: 18.8 us -> 39.3 us  [call(): pl.pallas_call(kernel, out_shape=out_shape, grid_spec=pltpu.PrefetchScala...]
    ppermute x4, starting transfers between devices: 19.9 us -> 4.03 us  [shift(): lax.ppermute(value, axis, [(i, (i + step) % count) for i in range(count)])]
    unnamed x56 -> x14, local copies, waits for them, and re-layouts: 17.4 us -> 3.63 us
    slice x1, local copies, waits for them, and re-layouts: 0.05 us -> 1.11 us  [on_device(): back = lax.ppermute(rest[:NB], 'span', swap)]
    ppermute x4, waiting for transfers between devices: 2.58 us -> 3.45 us  [shift(): lax.ppermute(value, axis, [(i, (i + step) % count) for i in range(count)])]
    slice x1, local copies, waits for them, and re-layouts: 0.01 us -> 0.83 us  [on_device(): from_north = shift(side[2], 'span', -1)]
    select_n x1, other arithmetic: 1.3 us -> 2.02 us  [on_device(): jnp.where(jnp.logical_and(takes, at >= offset_in), arrived, column_state[...]
  transfers between devices with their start and end apart: 6 -> 6, of which waited for: 2 -> 1; matrix products, arithmetic and copies ran while one was open for 5% -> 11% of each run, Pallas kernels for 22% -> 26%
where the time goes in v3:
time: 68.2 us; the launch traced here: 67.1 us
  Pallas kernels  39.3 us (58%)
  local copies, waits for them, and re-layouts  10.1 us (15%)
  between operations  5.77 us (8%)
  starting transfers between devices  4.67 us (7%)
  other arithmetic  3.86 us (6%)
  waiting for transfers between devices  3.45 us (5%)
    pallas_call x3, Pallas kernels, call(): pl.pallas_call(kernel, out_shape=out_shape, grid_spec=pltpu.PrefetchScala...  39.3 us
    ppermute x4, starting transfers between devices, shift(): lax.ppermute(value, axis, [(i, (i + step) % count) for i in range(count)])  4.03 us
    unnamed x14, local copies, waits for them, and re-layouts  3.63 us
    ppermute x4, waiting for transfers between devices, shift(): lax.ppermute(value, axis, [(i, (i + step) % count) for i in range(count)])  3.45 us
    select_n x1, other arithmetic, on_device(): jnp.where(jnp.logical_and(takes, at >= offset_in), arrived, column_state[...  2.02 us
    another operation x1, local copies, waits for them, and re-layouts, on_device(): edge_flat[:, None]  1.38 us
  transfers between devices with their start and end apart: 6, of which 1 were waited for; matrix products, arithmetic and copies ran while one was open for 11% of the time, Pallas kernels for 26%

profile of v3, /device:TPU:1, one launch (start us, length us, event | category | flops | bytes accessed | tf_op | source)
XLA Modules:
  0.0 67.1 jit_solution(3151784645104267653)
XLA Ops:
  0.0 1.3 %fusion.1 = (s32[1]{0:T(128)}, s32[1]{0:T(128)}) fusion(s32[32]{0:T(128)} %param.11, s32[]{:T(128)S(6)} %select_n.19, s32[]{:T(128)S(6)} %select_n.20), kind=kLoop, calls=%fused_computation.6 | loop fusion | bytes 24 | tf_op jit(solution)/shard_map/dynamic_slice | solution.py:310
  2.0 1.2 %constant_dynamic-slice_fusion = bf16[256,1152]{1,0:T(8,128)(2,1)S(1)} fusion(bf16[768,1152]{1,0:T(8,128)(2,1)} %last_ref.1, s32[]{:T(128)S(6)} %min.12), kind=kLoop, calls=%fused_computation.4 | loop fusion | bytes 1179652 | tf_op jit(solution)/shard_map/dynamic_slice | solution.py:320
  3.2 0.1 collective-permute-start
  8.4 1.4 %copy.12.refs_0_ = bf16[3,32,16]{2,1,0:T(8,128)(2,1)} copy(bf16[3,32,16]{1,2,0:T(8,128)(2,1)} %param.13) | data formatting | bytes 6144 | tf_op args[3]
  9.7 1.4 %broadcast_in_dim_reshape.8.place = s32[64,1]{1,0:T(8,128)} reshape(s32[1,4,16]{2,1,0:T(4,128)} %param.12) | data formatting | bytes 512 | tf_op jit(solution)/shard_map/broadcast_in_dim;reshape | solution.py:324
  11.1 1.4 %copy.13.refs_2_ = bf16[3,64,32]{2,1,0:T(8,128)(2,1)} copy(bf16[3,64,32]{1,2,0:T(8,128)(2,1)} %param.15) | data formatting | bytes 24576 | tf_op args[5]
  12.6 0.6 pad_add_fusion.1.sizes
  13.2 0.0 collective-permute-done
  13.2 2.0 %slice_select_fusion.x_ref = bf16[256,1152]{1,0:T(8,128)(2,1)} fusion(bf16[256,1152]{1,0:T(8,128)(2,1)S(1)} %collective-permute-done, bf16[768,1152]{1,0:T(8,128)(2,1)} %last_ref.1, pred[256]{0:T(512)(128)(4,1)S(1)} %compare_and_fusion), kind=kLoop, calls=%fused_computation | loop fusion | flops 294912 | bytes 1769728 | tf_op jit(solution)/shard_map/jit(_where)/select_n | solution.py:332
  15.2 17.8 %shard_map.101.rest = bf16[512,1152]{1,0:T(8,128)(2,1)} custom-call(s32[2]{0:T(128)} %pad_add_fusion.1.sizes, bf16[256,1152]{1,0:T(8,128)(2,1)} %slice_select_fusion.x_ref, bf16[768,1152]{1,0:T(8,128)(2,1)} %last_ref.1, bf16[3,32,16]{2,1,0:T(8,128)(2,1)} %copy.12.refs_0_, bf16[8,3,32,32]{3,2,1,0:T(8,128)(2,1)} %refs_1_.3, bf16[3,64,32]{2,1,0:T(8,128)(2,1)} %copy.13.refs_2_, ...), custom_call_target="tpu_custom_call" | custom-call | flops 20000000000 | bytes 4000000 | tf_op jit(solution)/shard_map/pallas_call | solution.py:244
  33.0 1.1 %slice.28 = bf16[256,1152]{1,0:T(8,128)(2,1)S(1)} slice(bf16[512,1152]{1,0:T(8,128)(2,1)} %shard_map.101.rest), slice={[0:256], [0:1152]} | slice | bytes 1179648 | tf_op jit(solution)/shard_map/slice | solution.py:338
  34.1 0.0 copy-start.5
  34.2 0.5 collective-permute-start.1
  34.7 17.5 %shard_map.100 = (bf16[256,1152]{1,0:T(8,128)(2,1)}, bf16[64,1152]{1,0:T(8,128)(2,1)}) custom-call(s32[1]{0:T(128)} %get-tuple-element.13.sizes, bf16[768,1152]{1,0:T(8,128)(2,1)} %last_ref.1, s32[64,1]{1,0:T(8,128)} %broadcast_in_dim_reshape.8.place, bf16[3,32,16]{2,1,0:T(8,128)(2,1)} %copy.12.refs_0_, bf16[8,3,32,32]{3,2,1,0:T(8,128)(2,1)} %refs_1_.3, ...), custom_call_target="tpu_custom_call" | custom-call | flops 15000000512 | bytes 4000000 | tf_op jit(solution)/shard_map/pallas_call | solution.py:244
  52.2 0.8 %fusion = (bf16[16,1152]{1,0:T(8,128)(2,1)S(1)}, bf16[16,1152]{1,0:T(8,128)(2,1)S(1)}, bf16[16,1152]{1,0:T(8,128)(2,1)S(1)}, bf16[16,1152]{1,0:T(8,128)(2,1)S(1)}) fusion(bf16[64,1152]{1,0:T(8,128)(2,1)} %get-tuple-element.8.edges), kind=kLoop, calls=%fused_computation.5 | loop fusion | bytes 294912 | tf_op jit(solution)/shard_map/slice | solution.py:329
  53.0 0.1 collective-permute-start.5
  53.2 2.1 %collective-permute-start.4 = (bf16[16,1152]{1,0:T(8,128)(2,1)S(1)}, bf16[16,1152]{1,0:T(8,128)(2,1)S(1)}, u32[]{:S(2)}, u32[]{:S(2)}) collective-permute-start(bf16[16,1152]{1,0:T(8,128)(2,1)S(1)} %get-tuple-element.10), channel_id=1, source_target_pairs={{0,1},{1,2},{2,3},{3,0},{4,5},{5,6},{6,7},{7,4},{8,9},{9,10},{10,1... | collective-permute-start | bytes 110600 | tf_op jit(solution)/shard_map/ppermute | solution.py:304
  55.3 1.8 %collective-permute-start.2 = (bf16[16,1152]{1,0:T(8,128)(2,1)S(1)}, bf16[16,1152]{1,0:T(8,128)(2,1)S(1)}, u32[]{:S(2)}, u32[]{:S(2)}) collective-permute-start(bf16[16,1152]{1,0:T(8,128)(2,1)S(1)} %get-tuple-element.12), channel_id=1, source_target_pairs={{0,4},{4,8},{8,12},{12,16},{16,20},{20,24},{24,28},{28,0},{1,5},{5... | collective-permute-start | bytes 110600 | tf_op jit(solution)/shard_map/ppermute | solution.py:304
  57.1 1.2 %pad_add_fusion.sizes = s32[3]{0:T(128)} fusion(s32[1]{0:T(128)} %bitcast.3, s32[1]{0:T(128)} %bitcast.2, s32[1]{0:T(128)} %get-tuple-element.13.sizes), kind=kLoop, calls=%fused_computation.2 | loop fusion | flops 6 | bytes 24 | tf_op jit(solution)/shard_map/stack | solution.py:339
  58.3 0.6 broadcast_in_dim_reshape.7.place
  58.9 3.4 %collective-permute-done.2.west = bf16[16,1152]{1,0:T(8,128)(2,1)S(1)} collective-permute-done((bf16[16,1152]{1,0:T(8,128)(2,1)S(1)}, bf16[16,1152]{1,0:T(8,128)(2,1)S(1)}, u32[]{:S(2)}, u32[]{:S(2)}) %collective-permute-start.2) | collective-permute-done | bytes 36896 | tf_op jit(solution)/shard_map/ppermute | solution.py:304
  62.4 0.6 copy-done.4
  63.0 0.2 copy-done
  63.2 3.9 %shard_map.102 = bf16[768,1152]{1,0:T(8,128)(2,1)} custom-call(s32[3]{0:T(128)} %pad_add_fusion.sizes, bf16[256,1152]{1,0:T(8,128)(2,1)} %get-tuple-element.7.y0, bf16[512,1152]{1,0:T(8,128)(2,1)} %shard_map.101.rest, bf16[256,1152]{1,0:T(8,128)(2,1)} %copy-done, s32[1,64]{1,0:T(1,128)} %broadcast_in_dim_reshape.7.place, ...), custom_call_target="tpu_custom_call" | custom-call | flops 100000000 | bytes 4000000 | tf_op jit(solution)/shard_map/pallas_call | solution.py:244
  (15 shorter events, 0.0 us)
Async XLA Ops:
  3.2 10.0 %collective-permute-start = (bf16[256,1152]{1,0:T(8,128)(2,1)S(1)}, bf16[256,1152]{1,0:T(8,128)(2,1)S(1)}, u32[]{:S(2)}, u32[]{:S(2)}) collective-permute-start(bf16[256,1152]{1,0:T(8,128)(2,1)S(1)} %constant_dynamic-slice_fusion), channel_id=1, source_target_pairs={{0,1},{1,0},{2,3},{3,2},{4,5},{5,4},{6,7},{7,6},{8,9},{9,8},{10,11... | collective-permute-start | bytes 1769480 | tf_op jit(solution)/shard_map/ppermute | solution.py:321
  34.1 24.1 %copy-start.5 = (s32[1,4,16]{2,1,0:T(4,128)S(1)}, s32[1,4,16]{2,1,0:T(4,128)}, u32[]{:S(2)}) copy-start(s32[1,4,16]{2,1,0:T(4,128)} %param.12) | copy-start | bytes 772
  34.2 28.2 %collective-permute-start.1 = (bf16[256,1152]{1,0:T(8,128)(2,1)S(1)}, bf16[256,1152]{1,0:T(8,128)(2,1)S(1)}, u32[]{:S(2)}, u32[]{:S(2)}) collective-permute-start(bf16[256,1152]{1,0:T(8,128)(2,1)S(1)} %slice.28), channel_id=1, source_target_pairs={{0,1},{1,0},{2,3},{3,2},{4,5},{5,4},{6,7},{7,6},{8,9},{9,8},{10,11... | collective-permute-start | bytes 1769480 | tf_op jit(solution)/shard_map/ppermute | solution.py:338
  53.0 5.9 %collective-permute-start.5 = (bf16[16,1152]{1,0:T(8,128)(2,1)S(1)}, bf16[16,1152]{1,0:T(8,128)(2,1)S(1)}, u32[]{:S(2)}, u32[]{:S(2)}) collective-permute-start(bf16[16,1152]{1,0:T(8,128)(2,1)S(1)} %get-tuple-element.9), channel_id=1, source_target_pairs={{0,3},{1,0},{2,1},{3,2},{4,7},{5,4},{6,5},{7,6},{8,11},{9,8},{10,9... | collective-permute-start | bytes 110600 | tf_op jit(solution)/shard_map/ppermute | solution.py:304
  53.2 5.7 %collective-permute-start.4 = (bf16[16,1152]{1,0:T(8,128)(2,1)S(1)}, bf16[16,1152]{1,0:T(8,128)(2,1)S(1)}, u32[]{:S(2)}, u32[]{:S(2)}) collective-permute-start(bf16[16,1152]{1,0:T(8,128)(2,1)S(1)} %get-tuple-element.10), channel_id=1, source_target_pairs={{0,1},{1,2},{2,3},{3,0},{4,5},{5,6},{6,7},{7,4},{8,9},{9,10},{10,1... | collective-permute-start | bytes 110600 | tf_op jit(solution)/shard_map/ppermute | solution.py:304
  55.3 3.6 %collective-permute-start.3 = (bf16[16,1152]{1,0:T(8,128)(2,1)S(1)}, bf16[16,1152]{1,0:T(8,128)(2,1)S(1)}, u32[]{:S(2)}, u32[]{:S(2)}) collective-permute-start(bf16[16,1152]{1,0:T(8,128)(2,1)S(1)} %get-tuple-element.11), channel_id=1, source_target_pairs={{0,28},{4,0},{8,4},{12,8},{16,12},{20,16},{24,20},{28,24},{1,29},{... | collective-permute-start | bytes 110600 | tf_op jit(solution)/shard_map/ppermute | solution.py:304
  55.3 7.1 %collective-permute-start.2 = (bf16[16,1152]{1,0:T(8,128)(2,1)S(1)}, bf16[16,1152]{1,0:T(8,128)(2,1)S(1)}, u32[]{:S(2)}, u32[]{:S(2)}) collective-permute-start(bf16[16,1152]{1,0:T(8,128)(2,1)S(1)} %get-tuple-element.12), channel_id=1, source_target_pairs={{0,4},{4,8},{8,12},{12,16},{16,20},{20,24},{24,28},{28,0},{1,5},{5... | collective-permute-start | bytes 110600 | tf_op jit(solution)/shard_map/ppermute | solution.py:304
  58.9 3.5 %copy-start.1 = (bf16[16,1152]{1,0:T(8,128)(2,1)}, bf16[16,1152]{1,0:T(8,128)(2,1)S(1)}, u32[]{:S(2)}) copy-start(bf16[16,1152]{1,0:T(8,128)(2,1)S(1)} %collective-permute-done.5.north) | copy-start | bytes 110596
  58.9 3.5 %copy-start.2 = (bf16[16,1152]{1,0:T(8,128)(2,1)}, bf16[16,1152]{1,0:T(8,128)(2,1)S(1)}, u32[]{:S(2)}) copy-start(bf16[16,1152]{1,0:T(8,128)(2,1)S(1)} %collective-permute-done.4.south) | copy-start | bytes 110596
  58.9 3.5 %copy-start.3 = (bf16[16,1152]{1,0:T(8,128)(2,1)}, bf16[16,1152]{1,0:T(8,128)(2,1)S(1)}, u32[]{:S(2)}) copy-start(bf16[16,1152]{1,0:T(8,128)(2,1)S(1)} %collective-permute-done.3.east) | copy-start | bytes 110596
  62.4 0.6 copy-start.4
  62.4 0.8 %copy-start = (bf16[256,1152]{1,0:T(8,128)(2,1)}, bf16[256,1152]{1,0:T(8,128)(2,1)S(1)}, u32[]{:S(2)}) copy-start(bf16[256,1152]{1,0:T(8,128)(2,1)S(1)} %collective-permute-done.1.back) | copy-start | bytes 1769476
